TPU v7x, 128 devices: a whole 4x4x4 slice. The times are simulated.
128 devices in a mesh: dst: 32 (over x, y, core), src: 4 (over z).
Axes of the slice: x: 4, y: 4, z: 4, core: 2. Of those that a mesh axis runs over, the one named last changes fastest.
Arguments:
- features: bfloat16 [32768, 512], P(('dst', 'src'))
- w_query: bfloat16 [512, 512], replicated
- w_key: bfloat16 [512, 512], replicated
- w_value: bfloat16 [512, 512], replicated, may hold values from -0.25 to 0.25
- w_out: bfloat16 [512, 512], replicated, may hold values from -0.25 to 0.25
- node_bits: int32 [32768], P('dst'), may hold values from 0 to 1073741823
- block_src: int32 [256, 4, 32], P('dst', 'src'), may hold values from 0 to 63, as said below
- block_count: int32 [256, 4], P('dst', 'src'), may hold values from 0 to 32, as said below
- graph_ids: int32 [32768], P(('dst', 'src')), may hold values from 0 to 3, as said below
Outputs:
- updated: bfloat16 [32768, 512], P(('dst', 'src'))
- pooled: float32 [4, 512], replicated
Inputs may be any that keep to these rules, and one draw needn't show every extreme that they name: For destination block b and group s only the first block_count[b, s] entries of block_src[b, s] are used; they are distinct blocks of the group, all in the graph of block b. The group that holds block b itself lists that block first. `block_count`: the group that holds a destination block lists 1 or more blocks for it. `graph_ids`: graph ids never fall along the nodes; every graph holds one or more whole blocks of 128 nodes.
All inputs are finite; a program needn't handle non-finite values.
Results may differ from a plain program's by a relative error of at most 0.0078.
Values may be sent and summed in bfloat16 or wider, within the bound.
A program may use at most 128 MiB of HBM per device.

v0:
```python
import math

import jax
import jax.numpy as jnp
from jax import lax
from jax.sharding import PartitionSpec as P

HEADS = 8
BLK = 128
GRAPHS = 4


NEG_FLOOR = -1e30


def merged_2(part, axis, combine):
    gathered = jax.tree.map(lambda a: lax.all_gather(a, axis), part)

    def take(source):
        return jax.tree.map(lambda a: lax.dynamic_index_in_dim(a, source, 0, False), gathered)

    return lax.fori_loop(
        1, lax.axis_size(axis), lambda source, state: combine(state, take(source)), take(0)
    )


def spread_heads(factor, head_depth):
    return jnp.repeat(factor, head_depth, axis=-1)


def shards(features, w_query, w_key, w_value, w_out, node_bits, block_src, block_count, graph_ids):
    shard_rows, model_width = features.shape
    src_total = lax.axis_size("src")
    dst_place = lax.axis_index("dst")
    src_place = lax.axis_index("src")
    head_depth = model_width // HEADS
    score_scale = 1.0 / math.sqrt(head_depth)
    per_shard = shard_rows // BLK
    slot_limit = block_src.shape[2]
    group_size = math.gcd(8, slot_limit)
    own_queries = jnp.dot(features, w_query, preferred_element_type=jnp.float32).astype(
        jnp.bfloat16
    )
    queries = lax.all_gather(own_queries, "src", axis=0, tiled=True)
    paired = jnp.concatenate([w_key, w_value], axis=1)
    key_value = jnp.dot(features, paired, preferred_element_type=jnp.float32).astype(jnp.bfloat16)
    gathered = lax.all_gather(key_value, "dst", axis=0, tiled=True)
    source_tiles = gathered.reshape(-1, BLK, 2 * model_width)
    dst_blocks = src_total * per_shard
    query_tiles = queries.reshape(dst_blocks, BLK, HEADS, head_depth)
    bit_tiles = node_bits.reshape(dst_blocks, BLK)
    slot_lists = block_src[:, 0, :]
    slot_counts = block_count[:, 0]
    lane_ids = jnp.arange(BLK, dtype=jnp.int32)

    def one_block(operands):
        query_tile, bit_row, slot_row, slot_total, block_place = operands
        dst_ids = dst_place * (src_total * shard_rows) + block_place * BLK + lane_ids

        def turn(turn_index, state_now):
            running_top, running_sum, running_acc = state_now
            first_slot = turn_index * group_size
            chosen = lax.dynamic_slice_in_dim(slot_row, first_slot, group_size)
            live_slot = first_slot + jnp.arange(group_size, dtype=jnp.int32) < slot_total
            fetched = jnp.take(source_tiles, chosen, axis=0)
            key_part = fetched[:, :, :model_width].reshape(group_size * BLK, HEADS, head_depth)
            value_part = fetched[:, :, model_width:].reshape(group_size * BLK, HEADS, head_depth)
            starts = (
                chosen // per_shard * src_total + src_place
            ) * shard_rows + chosen % per_shard * BLK
            src_ids = (starts[:, None] + lane_ids[None, :]).reshape(-1)
            bit_on = jnp.right_shift(bit_row[:, None], (src_ids % 30)[None, :]) & 1
            edge_mask = ((bit_on == 1) | (dst_ids[:, None] == src_ids[None, :])) & jnp.repeat(
                live_slot, BLK
            )[None, :]
            scores = (
                jnp.einsum("qhd,khd->qhk", query_tile, key_part, preferred_element_type=jnp.float32)
                * score_scale
            )
            masked = jnp.where(edge_mask[:, None, :], scores, NEG_FLOOR)
            new_top = jnp.maximum(running_top, jnp.max(masked, axis=-1))
            weights = jnp.where(edge_mask[:, None, :], jnp.exp(masked - new_top[:, :, None]), 0.0)
            factor = jnp.exp(running_top - new_top)
            new_sum = running_sum * factor + jnp.sum(weights, axis=-1)
            update = jnp.einsum(
                "qhk,khd->qhd",
                weights.astype(jnp.bfloat16),
                value_part,
                preferred_element_type=jnp.float32,
            )
            new_acc = running_acc * factor[:, :, None] + update
            return (new_top, new_sum, new_acc)

        initial = (
            jnp.full((BLK, HEADS), NEG_FLOOR, jnp.float32),
            jnp.zeros((BLK, HEADS), jnp.float32),
            jnp.zeros((BLK, HEADS, head_depth), jnp.float32),
        )
        turn_count = (slot_total + group_size - 1) // group_size
        block_top, block_sum, block_acc = lax.fori_loop(0, turn_count, turn, initial)
        return (block_top, block_sum, block_acc.reshape(BLK, model_width))

    part_top, part_sum, part_acc = lax.map(
        one_block,
        (query_tiles, bit_tiles, slot_lists, slot_counts, jnp.arange(dst_blocks, dtype=jnp.int32)),
    )
    part_top = part_top.reshape(-1, HEADS)
    part_sum = part_sum.reshape(-1, HEADS)
    part_acc = part_acc.reshape(-1, model_width)

    def merge_parts(earlier, later_part):
        top_a, sum_a, acc_a = earlier
        top_b, sum_b, acc_b = later_part
        joined_top = jnp.maximum(top_a, top_b)
        factor_a = jnp.exp(top_a - joined_top)
        factor_b = jnp.exp(top_b - joined_top)
        joined_sum = sum_a * factor_a + sum_b * factor_b
        joined_acc = acc_a * spread_heads(factor_a, head_depth) + acc_b * spread_heads(
            factor_b, head_depth
        )
        return (joined_top, joined_sum, joined_acc)

    merged = merged_2((part_top, part_sum, part_acc), "src", merge_parts)
    own_sum = lax.dynamic_slice_in_dim(merged[1], src_place * shard_rows, shard_rows, 0)
    own_acc = lax.dynamic_slice_in_dim(merged[2], src_place * shard_rows, shard_rows, 0)
    attention = (own_acc / spread_heads(own_sum, head_depth)).astype(jnp.bfloat16)
    mixed = jnp.dot(attention, w_out, preferred_element_type=jnp.float32)
    updated = (features.astype(jnp.float32) + mixed).astype(jnp.bfloat16)
    member = graph_ids[:, None] == jnp.arange(GRAPHS, dtype=jnp.int32)[None, :]
    graph_sums = lax.dot_general(
        member.astype(jnp.bfloat16),
        updated,
        (((0,), (0,)), ((), ())),
        preferred_element_type=jnp.float32,
    )
    node_counts = jnp.sum(member.astype(jnp.float32), axis=0)
    graph_sums, node_counts = lax.psum((graph_sums, node_counts), ("dst", "src"))
    pooled = graph_sums / jnp.sqrt(node_counts)[:, None]
    return (updated, pooled)


def solution(mesh):
    placed = (
        P(("dst", "src"), None),
        P(),
        P(),
        P(),
        P(),
        P("dst"),
        P("dst", "src", None),
        P("dst", "src"),
        P(("dst", "src")),
    )
    return jax.shard_map(
        shards,
        mesh=mesh,
        in_specs=placed,
        out_specs=(P(("dst", "src"), None), P()),
        check_vma=False,
    )
```

profile of v0, /device:TPU:1, one launch (start us, length us, event | category | flops | bytes accessed | tf_op | source)
XLA Modules:
  0.0 1035.2 jit_solution(17578148519930804152)
XLA Ops:
  8.2 2.0 convolution_convert_fusion.1
  10.2 2.6 fusion.26
  12.9 23.9 %all-gather.4.cloned.1.call-done = bf16[1024,512]{1,0:T(8,128)(2,1)} async-done(((bf16[256,512]{1,0:T(8,128)(2,1)}), bf16[1024,512]{1,0:T(8,128)(2,1)}) %all-gather.4.cloned.1.call-update) | async-done | bytes 1048592 | tf_op jit(solution)/shard_map/all_gather | solution.py:44
  36.8 2.8 reshape.181
  39.6 1.9 copy.41
  41.5 80.2 %all-gather.6.cloned.1.call-done = bf16[8192,1024]{0,1:T(8,128)(2,1)} async-done(((bf16[256,1024]{0,1:T(8,128)(2,1)}), bf16[8192,1024]{0,1:T(8,128)(2,1)}) %all-gather.6.cloned.1.call-update) | async-done | bytes 16777232 | tf_op jit(solution)/shard_map/all_gather | solution.py:47
  121.7 22.4 %copy.49 = bf16[8192,1024]{1,0:T(8,128)(2,1)} copy(bf16[8192,1024]{0,1:T(8,128)(2,1)} %all-gather.6.cloned.1.call-done) | data formatting | bytes 33554432
  144.1 133.9 %while.88 = (s32[]{:T(128)}, f32[8,128,8]{1,2,0:T(8,128)S(1)}, f32[8,128,8]{1,2,0:T(8,128)S(1)}, f32[8,128,512]{2,1,0:T(8,128)}, s32[8]{0:T(128)S(1)}, /*index=5...) while((s32[]{:T(128)}, f32[8,128,8]{1,2,0:T(8,128)S(1)}, ...), condition=%wide.region_5.6_spmd.clone.clone, body=%wide.region_0.5_spmd.clone.clone.sunk | while | flops 284044704 | bytes 55299948 | solution.py:103
  149.0 22.0 %while.89 = (s32[]{:T(128)}, f32[128,8]{0,1:T(8,128)S(1)}, f32[128,8]{0,1:T(8,128)S(1)}, f32[128,8,64]{0,2,1:T(8,128)S(1)}, s32[]{:T(128)}, /*index=5*/s32[128]{...) while((s32[]{:T(128)}, f32[128,8]{0,1:T(8,128)S(1)}, ...), condition=%wide.region_4.4_spmd, body=%wide.region_1.3_spmd.sunk | while | flops 284044544 | bytes 53699096 | solution.py:100
  150.9 6.5 gather_fusion
  158.9 1.7 copy.60
  160.6 1.3 reshape.188
  161.9 2.2 fusion.71
  167.4 3.6 fusion.73
  176.7 22.0 %while.89 = (s32[]{:T(128)}, f32[128,8]{0,1:T(8,128)S(1)}, f32[128,8]{0,1:T(8,128)S(1)}, f32[128,8,64]{0,2,1:T(8,128)S(1)}, s32[]{:T(128)}, /*index=5*/s32[128]{...) while((s32[]{:T(128)}, f32[128,8]{0,1:T(8,128)S(1)}, ...), condition=%wide.region_4.4_spmd, body=%wide.region_1.3_spmd.sunk | while | flops 284044544 | bytes 53699096 | solution.py:100
  178.7 6.5 gather_fusion
  186.6 1.7 copy.60
  188.3 1.3 reshape.188
  189.6 2.2 fusion.71
  195.1 3.6 fusion.73
  215.9 22.0 %while.89 = (s32[]{:T(128)}, f32[128,8]{0,1:T(8,128)S(1)}, f32[128,8]{0,1:T(8,128)S(1)}, f32[128,8,64]{0,2,1:T(8,128)S(1)}, s32[]{:T(128)}, /*index=5*/s32[128]{...) while((s32[]{:T(128)}, f32[128,8]{0,1:T(8,128)S(1)}, ...), condition=%wide.region_4.4_spmd, body=%wide.region_1.3_spmd.sunk | while | flops 284044544 | bytes 53699096 | solution.py:100
  217.9 6.5 gather_fusion
  225.9 1.7 copy.60
  227.6 1.3 reshape.188
  228.9 2.2 fusion.71
  234.3 3.6 fusion.73
  243.7 22.0 %while.89 = (s32[]{:T(128)}, f32[128,8]{0,1:T(8,128)S(1)}, f32[128,8]{0,1:T(8,128)S(1)}, f32[128,8,64]{0,2,1:T(8,128)S(1)}, s32[]{:T(128)}, /*index=5*/s32[128]{...) while((s32[]{:T(128)}, f32[128,8]{0,1:T(8,128)S(1)}, ...), condition=%wide.region_4.4_spmd, body=%wide.region_1.3_spmd.sunk | while | flops 284044544 | bytes 53699096 | solution.py:100
  245.7 6.5 gather_fusion
  253.6 1.7 copy.60
  256.6 2.2 fusion.71
  262.1 3.6 fusion.73
  278.8 53.1 %all_gather.18 = f32[4,1024,8]{1,2,0:T(8,128)S(1)} all-gather(f32[1,1024,8]{1,2,0:T(8,128)S(1)} %bitcast.137), channel_id=1, replica_groups=mesh['dst'=32,'src'=4] {'src'}, dimensions={0}, use_global_device_ids=true | all-gather | bytes 163840 | tf_op jit(solution)/shard_map/all_gather | solution.py:17
  331.9 9.1 all_gather.17
  341.0 589.8 %all-gather.8.cloned.1.call-done = f32[4,1024,512]{2,1,0:T(8,128)} async-done(((f32[1,1024,512]{2,1,0:T(8,128)}), f32[4,1024,512]{2,1,0:T(8,128)}) %all-gather.8.cloned.1.call-update) | async-done | bytes 8388624 | tf_op jit(solution)/shard_map/all_gather | solution.py:17
  930.7 1.8 slice_bitcast_fusion
  932.5 1.9 copy.44
  934.4 25.6 %while.86 = (s32[]{:T(128)}, f32[1024,8]{0,1:T(8,128)S(1)}, f32[1024,8]{0,1:T(8,128)S(1)}, f32[1024,512]{0,1:T(8,128)}, f32[4,1024,8]{1,2,0:T(8,128)S(1)}, /*ind...) while((s32[]{:T(128)}, f32[1024,8]{0,1:T(8,128)S(1)}, ...), condition=%wide.region_7.8_spmd, body=%wide.region_6.7_spmd.sunk | while | flops 1622021 | bytes 15007895 | solution.py:22
  934.4 3.1 constant_dynamic-slice_fusion.5
  937.5 1.9 copy.58
  939.5 3.5 fusion.61
  943.0 3.1 constant_dynamic-slice_fusion.5
  946.0 1.9 copy.58
  948.0 3.5 fusion.61
  951.5 3.1 constant_dynamic-slice_fusion.5
  954.6 1.9 copy.58
  956.5 3.5 fusion.61
  961.1 1.4 fusion.27
  962.6 65.3 %all-reduce = (f32[4,512]{1,0:T(4,128)S(1)}, f32[4]{0:T(128)S(1)}) all-reduce(f32[4,512]{1,0:T(4,128)S(1)} %fusion.32, f32[4]{0:T(128)S(1)} %convert_reduce_fusion), channel_id=1, replica_groups=mesh['dst'=32,'src'=4] {'dst','src'}, use_global_device_ids=true, to_apply=%region_8.9 | all-reduce | flops 2052 | bytes 16416 | tf_op jit(solution)/shard_map/psum | solution.py:137
  (210 shorter events, 67.2 us)
Async XLA Ops:
  7.2 1.1 copy-start
  7.2 29.7 %all-gather.4.cloned.1.call-start = ((), (), s32[]{:S(2)}) async-start(), calls=%async_computation | async-start | bytes 1310720 | tf_op jit(solution)/shard_map/all_gather | solution.py:44
  10.2 111.5 %all-gather.6.cloned.1.call-start = ((), (), s32[]{:S(2)}) async-start(), calls=%async_computation.1 | async-start | bytes 17301504 | tf_op jit(solution)/shard_map/all_gather | solution.py:47
  12.9 917.9 %all-gather.8.cloned.1.call-start = ((), (), s32[]{:S(2)}) async-start(), calls=%async_computation.2 | async-start | bytes 10485760 | tf_op jit(solution)/shard_map/all_gather | solution.py:17
  41.5 102.5 %copy-start.6 = (s32[8,1]{0,1:T(1,128)S(1)}, s32[8,1]{0,1:T(1,128)}, u32[]{:S(2)}) copy-start(s32[8,1]{0,1:T(1,128)} %param.22) | copy-start | bytes 100
  164.2 1.9 copy-start.2
  191.9 1.9 copy-start.2
  231.1 1.9 copy-start.2
  258.9 1.9 copy-start.2
  278.0 0.7 copy-start.5
  934.4 26.7 %copy-start.4 = (bf16[256,512]{1,0:T(8,128)(2,1)S(1)}, bf16[256,512]{1,0:T(8,128)(2,1)}, u32[]{:S(2)}) copy-start(bf16[256,512]{1,0:T(8,128)(2,1)} %param.15) | copy-start | bytes 786436
  959.9 68.7 %copy-start.1 = (bf16[512,512]{1,0:T(8,128)(2,1)S(1)}, bf16[512,512]{1,0:T(8,128)(2,1)}, u32[]{:S(2)}) copy-start(bf16[512,512]{1,0:T(8,128)(2,1)} %param.16) | copy-start | bytes 1572868
  962.5 66.2 %copy-start.3 = (bf16[256,512]{1,0:T(8,128)(2,1)}, bf16[256,512]{1,0:T(8,128)(2,1)S(1)}, u32[]{:S(2)}) copy-start(bf16[256,512]{1,0:T(8,128)(2,1)S(1)} %fusion.27) | copy-start | bytes 786436
Sparse Core Ops, SparseCore 0:
  10.3 26.4 all-gather.3
  39.0 82.6 all-gather.5
  278.2 652.5 all-gather.7
where the time goes:
time: 1040 us
  waiting for transfers between devices  694 us (67%)
  local copies, waits for them, and re-layouts  134 us (13%)
  blocking collectives  127 us (12%)
  matrix products  29.3 us (3%)
  other arithmetic  25 us (2%)
  between operations  13.8 us (1%)
  loops' own time  11.1 us (1%)
    all_gather x1, waiting for transfers between devices, merged_2(): gathered = jax.tree.map(lambda a: lax.all_gather(a, axis), part)  590 us
    all_gather x1, waiting for transfers between devices, shards(): gathered = lax.all_gather(key_value, 'dst', axis=0, tiled=True)  80.2 us
    psum x1, blocking collectives, shards(): lax.psum((graph_sums, node_counts), ('dst', 'src'))  65.3 us
    all_gather x2, blocking collectives, merged_2(): gathered = jax.tree.map(lambda a: lax.all_gather(a, axis), part)  62.1 us
    unnamed x14, local copies, waits for them, and re-layouts  25.9 us
    gather x4, local copies, waits for them, and re-layouts, turn(): fetched = jnp.take(source_tiles, chosen, axis=0)  25.8 us
    all_gather x1, waiting for transfers between devices, shards(): queries = lax.all_gather(own_queries, 'src', axis=0, tiled=True)  23.9 us
  transfers between devices with their start and end apart: 3, of which 3 were waited for; matrix products, arithmetic and copies ran while one was open for 1% of the time, Pallas kernels for 0%

commit v1 on v0

v1 whole, which is shorter than its diff:
```python
import functools

import jax
import jax.numpy as jnp
from jax import lax
from jax.experimental import pallas as pl
from jax.experimental.pallas import tpu as pltpu
from jax.sharding import PartitionSpec as P

MESH = pl.DeviceIdType.MESH
BF, F32, I32 = jnp.bfloat16, jnp.float32, jnp.int32
WIDTH, HEADS, HD, BLK, ROWS = 512, 8, 64, 128, 256
SLOTS = 32
OUT_MASK = -3e38
FLOOR = -1e30
RING = 4
NBUF = 4


def place():
    d = lax.axis_index("dst")
    return d // 8, (d // 2) % 4, d % 2, lax.axis_index("src")


def dst_index(x, y, core):
    return (x % 4) * 8 + (y % 4) * 2 + core


def flip(a, b):
    return a + b - 2 * a * b


def nt(a, b):
    return lax.dot_general(a, b, (((1,), (1,)), ((), ())), preferred_element_type=F32)


def gather_kernel(
    feat, wq, wk, wv, ints,
    kb, vt, q_out, ints_out, dq_out, self_score, self_value,
    fbuf, kk, vv, wqt, wkt, wvt, dq, got,
    ring_send, ring_recv, sib_send, sib_recv, z_send, z_recv, i_send, i_recv, out_sem,
):
    x, y, c, z = place()
    me = dst_index(x, y, c)
    sibling = dst_index(x, y, 1 - c)

    def blk(core, i, j):
        return dst_index(x + (1 - core) * i + core * j, y + core * i + (1 - core) * j, core)

    zup, zdown = (z + 1) % 4, (z + 3) % 4
    peers = [(dst_index(x + 1, y, c), z), (dst_index(x + 3, y, c), z), (me, zup), (me, zdown)]
    for dy in range(4):
        for dc in range(2):
            if dy or dc:
                peers.append((dst_index(x, y + dy, flip(c, dc)), z))
    fbuf[me] = feat[...]
    barrier = pltpu.get_barrier_semaphore()
    for peer in peers:
        pl.semaphore_signal(barrier, inc=1, device_id=peer, device_id_type=MESH)
    pl.semaphore_wait(barrier, len(peers))

    def remote(src, dst, send, recv, to):
        return pltpu.make_async_remote_copy(
            src_ref=src, dst_ref=dst, send_sem=send, recv_sem=recv, device_id=to, device_id_type=MESH
        )

    sent = []

    def go(copy):
        copy.start()
        sent.append(copy)

    def along(row, step):
        if row == 0:
            return (blk(c, step, 0), z)
        return (blk(c, 0, step), z)

    def full(row, i, step):
        b = blk(c, i, 0)
        s = 0 if step == 1 else 1
        go(remote(fbuf.at[b], fbuf.at[b], ring_send.at[row, s], ring_recv.at[row, s], along(row, step)))

    def fulls(row, i):
        full(row, i, 1)
        full(row, i, 3)

    def half_ref(row, i, at, part):
        b = blk(c, at, 0) if row == 0 else blk(c, i, at)
        return fbuf.at[b, pl.ds(part * BLK, BLK)]

    def forward(row, i):
        for part, frm, step in ((0, 3, 1), (1, 1, 3)):
            r = half_ref(row, i, frm, part)
            go(remote(r, r, ring_send.at[row, 2 + part], ring_recv.at[row, 2 + part], along(row, step)))

    def wait_full(row, i):
        for s, frm in ((0, 3), (1, 1)):
            b = blk(c, frm, 0) if row == 0 else blk(c, i, frm)
            remote(fbuf.at[b], fbuf.at[b], ring_send.at[row, s], ring_recv.at[row, s], (sibling, z)).wait_recv()

    def wait_half(row, i):
        for part in range(2):
            r = half_ref(row, i, 2, part)
            remote(r, r, ring_send.at[row, 2 + part], ring_recv.at[row, 2 + part], (sibling, z)).wait_recv()

    def share(i, j):
        b = blk(c, i, j)
        go(remote(fbuf.at[b], fbuf.at[b], sib_send.at[i, j], sib_recv.at[i, j], (sibling, z)))

    def wait_share(i, j):
        b = blk(1 - c, i, j)
        remote(fbuf.at[b], fbuf.at[b], sib_send.at[i, j], sib_recv.at[i, j], (sibling, z)).wait_recv()

    def store(b, n):
        return [
            pltpu.make_async_copy(kk.at[b], kb.at[b], out_sem.at[b, 0]),
            pltpu.make_async_copy(vv.at[b], vt.at[b], out_sem.at[b, 1]),
        ]

    def project(b):
        f = fbuf[b]
        kk[b] = jnp.dot(f, wk[...], preferred_element_type=F32).astype(BF)
        v = nt(wvt[...], f).astype(BF)
        vv[b, 0] = v[:, :BLK]
        vv[b, 1] = v[:, BLK:]
        for copy in store(b, 0):
            copy.start()

    def project_many(n, where):
        def body(e, carry):
            project(where(e))
            return carry

        lax.fori_loop(0, n, body, 0)

    fulls(0, 0)
    fulls(1, 0)
    share(0, 0)
    for dy in range(4):
        for dc in range(2):
            s = (2 * y + dy) % 4
            src = ints.at[2 * s + dc]
            slot = 2 * s + c
            if dy == 0 and dc == 0:
                local_ints = pltpu.make_async_copy(src, got.at[slot], i_recv.at[dy, dc])
                local_ints.start()
            else:
                go(
                    remote(
                        src, got.at[slot], i_send.at[dy, dc], i_recv.at[dy, dc],
                        (dst_index(x, y + dy, flip(c, dc)), z),
                    )
                )
    wvt[...] = wv[...].T
    wqt[...] = wq[...].T
    wkt[...] = wk[...].T
    project(me)

    wait_full(0, 0)
    forward(0, 0)
    fulls(4, 3)
    fulls(2, 1)
    share(3, 0)
    share(1, 0)
    wait_full(1, 0)
    forward(1, 0)
    share(0, 3)
    share(0, 1)
    project_many(4, lambda e: blk(c, (1 - e // 2) * (1 + 2 * e), (e // 2) * (2 * e - 3)))
    wait_share(0, 0)
    project(sibling)

    wait_half(0, 0)
    fulls(3, 2)
    share(2, 0)
    wait_half(1, 0)
    share(0, 2)
    project_many(2, lambda e: blk(c, 2 - 2 * e, 2 * e))
    for i, j in ((1, 0), (3, 0), (0, 1), (0, 3)):
        wait_share(i, j)
    project_many(4, lambda e: blk(1 - c, (1 - e // 2) * (1 + 2 * e), (e // 2) * (2 * e - 3)))
    wait_share(2, 0)
    wait_share(0, 2)

    yy = (z - y + 4) % 4

    def plane_rows(cc):
        return fbuf.at[dst_index(x, yy, cc), pl.ds(pl.multiple_of(flip(c, cc) * BLK, BLK), BLK)]

    for up, to in ((0, zup), (1, zdown)):
        for cc in range(2):
            go(remote(plane_rows(cc), dq.at[z, cc], z_send.at[up, cc], z_recv.at[up, cc], (me, to)))
    own_copies = [pltpu.make_async_copy(plane_rows(cc), dq.at[z, cc], z_recv.at[3, cc]) for cc in range(2)]
    for copy in own_copies:
        copy.start()

    wait_full(4, 3)
    forward(4, 3)
    share(3, 3)
    share(3, 1)
    wait_full(2, 1)
    forward(2, 1)
    share(1, 3)
    share(1, 1)
    project_many(4, lambda e: blk(c, 1 + 2 * (e // 2), 1 + 2 * (e % 2)))
    project_many(2, lambda e: blk(1 - c, 2 - 2 * e, 2 * e))

    wait_half(4, 3)
    share(3, 2)
    wait_half(2, 1)
    share(1, 2)
    for up, frm in ((0, zdown), (1, zup)):
        for cc in range(2):
            remote(dq.at[frm, cc], dq.at[frm, cc], z_send.at[up, cc], z_recv.at[up, cc], (me, zup)).wait_recv()
    for cc, frm, to in ((0, zdown, zup), (1, zup, zdown)):
        go(remote(dq.at[frm, cc], dq.at[frm, cc], z_send.at[2, cc], z_recv.at[2, cc], (me, to)))
    project_many(2, lambda e: blk(c, 1 + 2 * e, 2))
    for i in (1, 3):
        for j in (1, 3):
            wait_share(i, j)
    project_many(4, lambda e: blk(1 - c, 1 + 2 * (e // 2), 1 + 2 * (e % 2)))

    wait_full(3, 2)
    forward(3, 2)
    share(2, 3)
    share(2, 1)
    project_many(2, lambda e: blk(c, 2, 1 + 2 * e))
    wait_share(1, 2)
    wait_share(3, 2)
    project_many(2, lambda e: blk(1 - c, 1 + 2 * e, 2))
    for copy in own_copies:
        copy.wait()

    def query(s, cc):
        q = nt(wqt[...], dq[s, cc]).astype(BF)
        q_out[2 * s + cc] = q * 0.125

    def queries(e, carry):
        query((z + 3 + e // 2) % 4, e % 2)
        return carry

    lax.fori_loop(0, 6, queries, 0)
    for cc in range(2):
        f = dq[z, cc]
        dq_out[cc] = f
        k = nt(wkt[...], f).astype(BF).astype(F32)
        q = q_out[2 * z + cc].astype(F32)
        prod = k * q
        self_score[cc] = jnp.concatenate(
            [jnp.sum(prod[h * HD : (h + 1) * HD], axis=0, keepdims=True) for h in range(HEADS)], axis=0
        )
        self_value[cc] = nt(wvt[...], f).astype(BF)
    local_ints.wait()
    for dy in range(4):
        for dc in range(2):
            if dy or dc:
                slot = 2 * ((2 * y + 4 - dy) % 4) + flip(c, dc)
                remote(
                    got.at[slot], got.at[slot], i_send.at[dy, dc], i_recv.at[dy, dc], (sibling, z)
                ).wait_recv()
    ints_out[...] = got[...]

    wait_half(3, 2)
    share(2, 2)
    project(blk(c, 2, 2))
    wait_share(2, 1)
    wait_share(2, 3)
    project_many(2, lambda e: blk(1 - c, 2, 1 + 2 * e))
    far = (z + 2) % 4
    for cc in range(2):
        remote(dq.at[far, cc], dq.at[far, cc], z_send.at[2, cc], z_recv.at[2, cc], (me, zup)).wait_recv()
    for cc in range(2):
        query(far, cc)
    wait_share(2, 2)
    project(blk(1 - c, 2, 2))

    def drain(b, carry):
        for copy in store(b, 0):
            copy.wait()
        return carry

    lax.fori_loop(0, 32, drain, 0)
    for copy in sent:
        copy.wait_send()


def gather_call(feat, wq, wk, wv, ints):
    vm = pl.BlockSpec(memory_space=pltpu.VMEM)
    anyw = pl.BlockSpec(memory_space=pl.ANY)
    dma = pltpu.SemaphoreType.DMA
    return pl.pallas_call(
        gather_kernel,
        out_shape=(
            jax.ShapeDtypeStruct((32, ROWS, WIDTH), BF),
            jax.ShapeDtypeStruct((32, 2, WIDTH, BLK), BF),
            jax.ShapeDtypeStruct((8, WIDTH, BLK), BF),
            jax.ShapeDtypeStruct((8, 8, BLK), I32),
            jax.ShapeDtypeStruct((2, BLK, WIDTH), BF),
            jax.ShapeDtypeStruct((2, HEADS, BLK), F32),
            jax.ShapeDtypeStruct((2, WIDTH, BLK), BF),
        ),
        in_specs=[vm] * 5,
        out_specs=(anyw, anyw, vm, vm, vm, vm, vm),
        scratch_shapes=[
            pltpu.VMEM((32, ROWS, WIDTH), BF),
            pltpu.VMEM((32, ROWS, WIDTH), BF),
            pltpu.VMEM((32, 2, WIDTH, BLK), BF),
            pltpu.VMEM((WIDTH, WIDTH), BF),
            pltpu.VMEM((WIDTH, WIDTH), BF),
            pltpu.VMEM((WIDTH, WIDTH), BF),
            pltpu.VMEM((4, 2, BLK, WIDTH), BF),
            pltpu.VMEM((8, 8, BLK), I32),
            dma((5, 4)), dma((5, 4)), dma((4, 4)), dma((4, 4)),
            dma((3, 2)), dma((4, 2)), dma((4, 2)), dma((4, 2)), dma((32, 2)),
        ],
        compiler_params=pltpu.CompilerParams(
            collective_id=0, has_side_effects=True, vmem_limit_bytes=56 << 20
        ),
        name="gather_project",
    )(feat, wq, wk, wv, ints)


def attention_kernel(
    lists, where_ref, qt, bits, self_score, self_value, kb, vt,
    acc_out, stat_out,
    et, rhs, acc, m, l, kbuf, vbuf, sem, sched, sx, sy,
):
    z = where_ref[0]
    base = where_ref[1]
    lane = lax.broadcasted_iota(I32, (BLK, BLK), 1)
    row = lax.broadcasted_iota(I32, (BLK, BLK), 0)
    for ph in range(15):
        et[ph] = jnp.where((row + 2 * ph) % 30 == lane, 1.0, 0.0).astype(BF)
    et[15] = jnp.where(lane == 31, 1.0, 0.0).astype(BF)

    def phase(g):
        return (4 * ((g // 2) * 8 + 2 * z + g % 2)) % 15

    def build(b, n):
        count = lists[b, 1, SLOTS]

        def inner(t, n):
            first = lists[b, 1, 2 * t]
            live = 2 * t + 1 < count
            second = jnp.where(live, lists[b, 1, jnp.minimum(2 * t + 1, SLOTS - 1)], first)
            sched[0, n] = b
            sched[1, n] = first
            sched[2, n] = second
            sched[3, n] = phase(first)
            sched[4, n] = jnp.where(live, phase(second), 15)
            return n + 1

        return lax.fori_loop(0, (count + 1) // 2, inner, n)

    steps = lax.fori_loop(0, 8, build, 0)
    for extra in range(2):
        for f in range(5):
            sched[f, steps + extra] = 15 if f >= 3 else 0
    even = 2 * ((steps + 1) // 2)

    def copies(i):
        slot = lax.rem(i, NBUF)
        a, b = sched[1, i], sched[2, i]
        return [
            pltpu.make_async_copy(kb.at[a], kbuf.at[slot, 0], sem.at[slot, 0]),
            pltpu.make_async_copy(kb.at[b], kbuf.at[slot, 1], sem.at[slot, 1]),
            pltpu.make_async_copy(vt.at[a], vbuf.at[slot, 0], sem.at[slot, 2]),
            pltpu.make_async_copy(vt.at[b], vbuf.at[slot, 1], sem.at[slot, 3]),
        ]

    for i in range(NBUF - 1):

        @pl.when(i <= even)
        def _():
            for copy in copies(i):
                copy.start()

    def prepare(b, carry):
        brow = bits[b, 0:1, :]
        rr = lax.broadcasted_iota(I32, (32, BLK), 0)
        on = (jnp.broadcast_to(brow, (32, BLK)) >> rr) & 1
        g = jnp.where(on == 1, 0.0, OUT_MASK)
        g = jnp.where(rr < 30, g, jnp.where(rr == 31, OUT_MASK, 0.0)).astype(BF)
        gg = jnp.concatenate([g, g], 1)
        z64 = jnp.zeros((HD, BLK), BF)
        for p in range(4):
            rhs[b, p, 0:64, 0:128] = qt[b, 128 * p : 128 * p + 64, :]
            rhs[b, p, 0:64, 128:256] = z64
            rhs[b, p, 64:128, 0:128] = z64
            rhs[b, p, 64:128, 128:256] = qt[b, 128 * p + 64 : 128 * p + 128, :]
            rhs[b, p, 128:160, :] = gg
            rhs[b, p, 160:256, :] = jnp.zeros((96, 256), BF)
        m[b] = jnp.full((HEADS, BLK), FLOOR, F32)
        l[b] = jnp.zeros((HEADS, BLK), F32)
        acc[b] = jnp.zeros((WIDTH, BLK), F32)
        return carry

    lax.fori_loop(0, 8, prepare, 0)
    for cc in range(2):
        b = 2 * z + cc
        start = where_ref[2 + cc] * BLK
        lanes = lax.broadcasted_iota(I32, (1, BLK), 1)
        on = (bits[b, 0:1, :] >> ((start + lanes) % 30)) & 1
        extra = jnp.broadcast_to(on, (HEADS, BLK)) == 0
        m[b] = jnp.where(extra, self_score[cc], FLOOR)
        l[b] = jnp.where(extra, 1.0, 0.0)
        acc[b] = jnp.where(
            jnp.broadcast_to(on, (WIDTH, BLK)) == 0, self_value[cc].astype(F32), 0.0
        )

    def scores(i, out, p):
        slot = lax.rem(i, NBUF)
        e0, e1, b = et[sched[3, i]], et[sched[4, i]], sched[0, i]
        k0 = kbuf[slot, 0, :, 128 * p : 128 * p + 128]
        k1 = kbuf[slot, 1, :, 128 * p : 128 * p + 128]
        lhs = jnp.concatenate([jnp.concatenate([k0, e0], 1), jnp.concatenate([k1, e1], 1)], 0)
        out[p] = jnp.dot(lhs, rhs[b, p], preferred_element_type=F32)

    def head(i, cur, h):
        slot, b = lax.rem(i, NBUF), sched[0, i]
        p, side = h // 2, h % 2
        old = m[b, h : h + 1, :]
        s = cur[p, :, 128 * side : 128 * side + 128]
        top = jnp.maximum(old, jnp.max(s, axis=0, keepdims=True))
        factor = jnp.exp(old - top)
        w = jnp.exp(cur[p, :, 128 * side : 128 * side + 128] - top)
        m[b, h : h + 1, :] = top
        l[b, h : h + 1, :] = l[b, h : h + 1, :] * factor + jnp.sum(w, axis=0, keepdims=True)
        rows = slice(64 * h, 64 * h + 64)
        v = jnp.concatenate([vbuf[slot, 0, rows, :], vbuf[slot, 1, rows, :]], 1)
        o = jnp.dot(v, w.astype(BF), preferred_element_type=F32)
        acc[b, rows, :] = acc[b, rows, :] * factor + o

    def wait(i):
        for copy in copies(i):
            copy.wait()

    def step(i, cur, nxt):
        @pl.when(i + NBUF - 1 <= even)
        def _():
            for copy in copies(i + NBUF - 1):
                copy.start()

        wait(i + 1)
        for p in range(4):
            scores(i + 1, nxt, p)
            head(i, cur, 2 * p)
            head(i, cur, 2 * p + 1)

    wait(0)
    for p in range(4):
        scores(0, sx, p)

    def body(j, carry):
        step(2 * j, sx, sy)
        step(2 * j + 1, sy, sx)
        return carry

    lax.fori_loop(0, even // 2, body, 0)
    acc_out[...] = acc[...].astype(BF)
    stat_out[:, 0:8, :] = m[...]
    stat_out[:, 8:16, :] = l[...]


def attention_call(ints, where, qt, self_score, self_value, kb, vt):
    vm = pl.BlockSpec(memory_space=pltpu.VMEM)
    sm = pl.BlockSpec(memory_space=pltpu.SMEM)
    anyw = pl.BlockSpec(memory_space=pl.ANY)
    return pl.pallas_call(
        attention_kernel,
        out_shape=(
            jax.ShapeDtypeStruct((8, WIDTH, BLK), BF),
            jax.ShapeDtypeStruct((8, 16, BLK), F32),
        ),
        in_specs=[sm, sm, vm, vm, vm, vm, anyw, anyw],
        out_specs=(vm, vm),
        scratch_shapes=[
            pltpu.VMEM((16, BLK, BLK), BF),
            pltpu.VMEM((8, 4, 256, 256), BF),
            pltpu.VMEM((8, WIDTH, BLK), F32),
            pltpu.VMEM((8, HEADS, BLK), F32),
            pltpu.VMEM((8, HEADS, BLK), F32),
            pltpu.VMEM((NBUF, 2, BLK, WIDTH), BF),
            pltpu.VMEM((NBUF, 2, WIDTH, BLK), BF),
            pltpu.SemaphoreType.DMA((NBUF, 4)),
            pltpu.SMEM((5, 136), I32),
            pltpu.VMEM((4, 256, 256), F32),
            pltpu.VMEM((4, 256, 256), F32),
        ],
        compiler_params=pltpu.CompilerParams(vmem_limit_bytes=56 << 20),
        name="block_attention",
    )(ints, where, qt, ints, self_score, self_value, kb, vt)


def merge_kernel(
    acc, stat, dq, ids, w_out,
    updated_out, pooled_out,
    acc_got, stat_got, made, mine, part, ring_part, total, all_part,
    a_send, a_recv, s_send, s_recv, u_send, u_recv, r_send, r_recv, g_send, g_recv,
):
    x, y, c, z = place()
    me = dst_index(x, y, c)
    ring = []
    for dy in range(4):
        for dc in range(2):
            if dy or dc:
                ring.append((dy, dc, (dst_index(x, y + dy, flip(c, dc)), z)))
    far = []
    for dx in range(4):
        for dz in range(4):
            if dx or dz:
                far.append((dx, dz, (dst_index(x + dx, y, c), (z + dz) % 4)))
    barrier = pltpu.get_barrier_semaphore()
    for _, _, peer in ring + far:
        pl.semaphore_signal(barrier, inc=1, device_id=peer, device_id_type=MESH)
    pl.semaphore_wait(barrier, len(ring) + len(far))

    def remote(src, dst, send, recv, to):
        return pltpu.make_async_remote_copy(
            src_ref=src, dst_ref=dst, send_sem=send, recv_sem=recv, device_id=to, device_id_type=MESH
        )

    sent = []

    def go(copy):
        copy.start()
        sent.append(copy)

    for dz in (2, 1, 3):
        to = (z + dz) % 4
        rows = pl.ds(2 * to, 2)
        go(remote(acc.at[rows], acc_got.at[dz - 1], a_send.at[dz - 1], a_recv.at[dz - 1], (me, to)))
        go(remote(stat.at[rows], stat_got.at[dz - 1], s_send.at[dz - 1], s_recv.at[dz - 1], (me, to)))
    for dz in (1, 3, 2):
        rows = pl.ds(2 * z, 2)
        remote(acc.at[rows], acc_got.at[dz - 1], a_send.at[dz - 1], a_recv.at[dz - 1], (me, z)).wait_recv()
        remote(stat.at[rows], stat_got.at[dz - 1], s_send.at[dz - 1], s_recv.at[dz - 1], (me, z)).wait_recv()
    yy = (z - y + 4) % 4
    for cc in range(2):
        b = 2 * z + cc
        stats = [stat[b]] + [stat_got[k, cc] for k in range(3)]
        top = stats[0][0:8]
        for s in stats[1:]:
            top = jnp.maximum(top, s[0:8])
        factors = [jnp.exp(s[0:8] - top) for s in stats]
        whole = sum(f * s[8:16] for f, s in zip(factors, stats))
        inv = 1.0 / whole
        factors = [f * inv for f in factors]
        pieces = []
        for h in range(HEADS):
            rows = slice(64 * h, 64 * h + 64)
            o = acc[b, rows, :].astype(F32) * factors[0][h : h + 1, :]
            for k in range(3):
                o = o + acc_got[k, cc, rows, :].astype(F32) * factors[k + 1][h : h + 1, :]
            pieces.append(o)
        att = jnp.concatenate(pieces, 0).T.astype(BF)
        mixed = jnp.dot(att, w_out[...], preferred_element_type=F32)
        new = (dq[cc].astype(F32) + mixed).astype(BF)
        made[cc] = new
        gid = ids[b, 2:3, :]
        member = jnp.where(
            jnp.broadcast_to(gid, (8, BLK)) == lax.broadcasted_iota(I32, (8, BLK), 0), 1.0, 0.0
        )
        sums = jnp.dot(member.astype(BF), new, preferred_element_type=F32)
        counts = jnp.broadcast_to(jnp.sum(member, axis=1, keepdims=True), (8, BLK))
        both = jnp.concatenate([sums, counts], 1)
        part[...] = both if cc == 0 else part[...] + both
    for cc in range(2):
        own = jnp.logical_and(yy == y, c == cc)
        half = flip(c, cc)
        copy = remote(made.at[cc], mine.at[half], u_send.at[cc], u_recv.at[half], (dst_index(x, yy, cc), z))
        local = pltpu.make_async_copy(made.at[cc], mine.at[half], u_recv.at[half])
        pl.when(jnp.logical_not(own))(copy.start)
        pl.when(own)(local.start)
    for dy, dc, to in ring:
        k = 2 * dy + dc
        go(remote(part, ring_part.at[k], r_send.at[k], r_recv.at[k], to))
    whole = part[...]
    for dy, dc, to in ring:
        k = 2 * dy + dc
        remote(part, ring_part.at[k], r_send.at[k], r_recv.at[k], to).wait_recv()
        whole = whole + ring_part[k]
    total[...] = whole
    for dx, dz, to in far:
        k = 4 * dx + dz
        go(remote(total, all_part.at[k], g_send.at[k], g_recv.at[k], to))
    for half in range(2):
        pltpu.make_async_copy(made.at[half], mine.at[half], u_recv.at[half]).wait()
    updated_out[0:BLK, :] = mine[0]
    updated_out[BLK:ROWS, :] = mine[1]
    for dx, dz, to in far:
        k = 4 * dx + dz
        remote(total, all_part.at[k], g_send.at[k], g_recv.at[k], to).wait_recv()
        whole = whole + all_part[k]
    scale = 1.0 / jnp.sqrt(jnp.concatenate([whole[0:4, WIDTH:]] * 4, 1))
    pooled_out[...] = whole[0:4, :WIDTH] * scale
    for cc in range(2):
        own = jnp.logical_and(yy == y, c == cc)
        copy = remote(
            made.at[cc], mine.at[flip(c, cc)], u_send.at[cc], u_recv.at[flip(c, cc)],
            (dst_index(x, yy, cc), z),
        )
        pl.when(jnp.logical_not(own))(copy.wait_send)
    for copy in sent:
        copy.wait_send()


def merge_call(acc, stat, dq, ids, w_out):
    vm = pl.BlockSpec(memory_space=pltpu.VMEM)
    dma = pltpu.SemaphoreType.DMA
    return pl.pallas_call(
        merge_kernel,
        out_shape=(
            jax.ShapeDtypeStruct((ROWS, WIDTH), BF),
            jax.ShapeDtypeStruct((4, WIDTH), F32),
        ),
        in_specs=[vm] * 5,
        out_specs=(vm, vm),
        scratch_shapes=[
            pltpu.VMEM((3, 2, WIDTH, BLK), BF),
            pltpu.VMEM((3, 2, 16, BLK), F32),
            pltpu.VMEM((2, BLK, WIDTH), BF),
            pltpu.VMEM((2, BLK, WIDTH), BF),
            pltpu.VMEM((8, WIDTH + BLK), F32),
            pltpu.VMEM((8, 8, WIDTH + BLK), F32),
            pltpu.VMEM((8, WIDTH + BLK), F32),
            pltpu.VMEM((16, 8, WIDTH + BLK), F32),
            dma((3,)), dma((3,)), dma((3,)), dma((3,)), dma((2,)), dma((2,)),
            dma((8,)), dma((8,)), dma((16,)), dma((16,)),
        ],
        compiler_params=pltpu.CompilerParams(
            collective_id=1, has_side_effects=True, vmem_limit_bytes=40 << 20
        ),
        name="merge_project_pool",
    )(acc, stat, dq, ids, w_out)


def shards(features, w_query, w_key, w_value, w_out, node_bits, block_src, block_count, graph_ids):
    x, y, c, z = place()
    bits = node_bits.reshape(8, 1, BLK)
    slots = jnp.concatenate(
        [block_src, jnp.broadcast_to(block_count[:, :, None], (8, 1, BLK - SLOTS))], axis=2
    )
    ids = jnp.tile(graph_ids.reshape(2, 1, BLK), (4, 1, 1))
    ints = jnp.concatenate([bits, slots, ids, jnp.zeros((8, 5, BLK), I32)], axis=1)
    kb, vt, qt, got, dq, self_score, self_value = gather_call(features, w_query, w_key, w_value, ints)
    yy = (z - y + 4) % 4
    own = [dst_index(x, yy, cc) * 8 + 2 * z + flip(c, cc) for cc in range(2)]
    where = jnp.stack([z, z, own[0], own[1]]).astype(I32)
    acc, stat = attention_call(
        got, where, qt, self_score, self_value, kb.reshape(64, BLK, WIDTH), vt.reshape(64, WIDTH, BLK)
    )
    return merge_call(acc, stat, dq, got, w_out)


def solution(mesh):
    placed = (
        P(("dst", "src"), None),
        P(),
        P(),
        P(),
        P(),
        P("dst"),
        P("dst", "src", None),
        P("dst", "src"),
        P(("dst", "src")),
    )
    return jax.shard_map(
        shards,
        mesh=mesh,
        in_specs=placed,
        out_specs=(P(("dst", "src"), None), P()),
        check_vma=False,
    )
```

time: 1040 us -> 125 us (0.12)
  waiting for transfers between devices: 694 us -> 0 us
  local copies, waits for them, and re-layouts: 134 us -> 4.86 us
  blocking collectives: 127 us -> 0 us
  Pallas kernels: 0 us -> 116 us
  matrix products: 29.3 us -> 0 us
  other arithmetic: 25 us -> 2.07 us
  between operations: 13.8 us -> 0.81 us
  loops' own time: 11.1 us -> 0 us
    all_gather x3 -> x0, waiting for transfers between devices: 694 us -> none  [the longest x1 590 us: merged_2(): gathered = jax.tree.map(lambda a: lax.all_gather(a, axis), part)]
    pallas_call x0 -> x3, Pallas kernels: none -> 116 us  [the longest x1 51.8 us: gather_call(): pl.pallas_call(gather_kernel, out_shape=(jax.ShapeDtypeStruct((32, ROWS,...]
    psum x1 -> x0, blocking collectives: 65.3 us -> none  [shards(): lax.psum((graph_sums, node_counts), ('dst', 'src'))]
    all_gather x2 -> x0, blocking collectives: 62.1 us -> none  [merged_2(): gathered = jax.tree.map(lambda a: lax.all_gather(a, axis), part)]
    dot_general x12 -> x0, matrix products: 29.3 us -> none  [the longest x4 14.2 us: turn(): jnp.einsum('qhk,khd->qhd', weights.astype(jnp.bfloat16), value_part, pref...]
    gather x4 -> x0, local copies, waits for them, and re-layouts: 25.8 us -> none  [turn(): fetched = jnp.take(source_tiles, chosen, axis=0)]
    dynamic_slice x23 -> x0, local copies, waits for them, and re-layouts: 25 us -> none  [the longest x6 15.1 us: take(): lax.dynamic_index_in_dim(a, source, 0, False)]
    unnamed x14 -> x12, local copies, waits for them, and re-layouts: 25.9 us -> 3.37 us
  transfers between devices with their start and end apart: 3 -> 0, of which waited for: 3 -> 0; matrix products, arithmetic and copies ran while one was open for 1% -> 0% of each run, Pallas kernels for 0% -> 0%
where the time goes in v1:
time: 125 us; the launch traced here: 124 us
  Pallas kernels  116 us (93%)
  local copies, waits for them, and re-layouts  4.86 us (4%)
  other arithmetic  2.07 us (2%)
    pallas_call x1, Pallas kernels, gather_call(): pl.pallas_call(gather_kernel, out_shape=(jax.ShapeDtypeStruct((32, ROWS,...  51.8 us
    pallas_call x1, Pallas kernels, merge_call(): pl.pallas_call(merge_kernel, out_shape=(jax.ShapeDtypeStruct((ROWS, WIDTH...  46.2 us
    pallas_call x1, Pallas kernels, attention_call(): pl.pallas_call(attention_kernel, out_shape=(jax.ShapeDtypeStruct((8, WIDT...  18.4 us
    unnamed x12, local copies, waits for them, and re-layouts  3.37 us

profile of v1, /device:TPU:1, one launch (start us, length us, event | category | flops | bytes accessed | tf_op | source)
XLA Modules:
  0.0 124.2 jit_solution(14064715225615728468)
XLA Ops:
  0.7 0.7 pad_add_fusion.where_ref
  1.4 0.1 pad.8.clone
  1.5 0.7 broadcast_in_dim.12
  2.2 0.7 tile.11
  2.9 1.4 %add_add_fusion.ints = s32[8,8,128]{2,1,0:T(8,128)} fusion(s32[8,1,128]{2,1,0:T(1,128)S(1)} %bitcast.11, s32[8,1,96]{2,1,0:T(1,128)S(1)} %broadcast_in_dim.12, s32[8,1,32]{2,1,0:T(1,128)} %param.15, s32[8,1,128]{2,1,0:T(1,128)} %bitcast.12, s32[8]{0:T(128)S(1)} %pad.8.clone), kind=kLoop, calls=%fused_computation | loop fusion | flops 32768 | bytes 45088 | tf_op jit(solution)/shard_map/concatenate | solution.py:645
  4.3 51.8 %gather_project.1 = (bf16[32,256,512]{2,1,0:T(8,128)(2,1)}, bf16[32,2,512,128]{3,2,1,0:T(8,128)(2,1)}, bf16[8,512,128]{2,1,0:T(8,128)(2,1)}, s32[8,8,128]{2,1,0:...) custom-call(bf16[256,512]{1,0:T(8,128)(2,1)} %feat.1, ...), custom_call_target="tpu_custom_call" | custom-call | tf_op jit(solution)/shard_map/gather_project/pallas_call | solution.py:291
  56.1 0.0 copy-start.1
  56.1 0.0 copy-start.2
  56.1 0.0 copy-start.3
  56.1 18.4 %block_attention.1 = (bf16[8,512,128]{2,1,0:T(8,128)(2,1)}, f32[8,16,128]{2,1,0:T(8,128)}) custom-call(s32[8,8,128]{2,1,0:T(8,128)} %get-tuple-element.11.lists.bits.ids, s32[4]{0:T(128)} %pad_add_fusion.where_ref, bf16[8,512,128]{2,1,0:T(8,128)(2,1)} %get-tuple-element.12.qt, s32[8,8,128]{2,1,0:T(8,128)} %get-tuple-element.11.lists.bits.ids, ...), custom_call_target="tpu_custom_call" | custom-call | tf_op jit(solution)/shard_map/block_attention/pallas_call | solution.py:469
  74.5 0.0 copy-done.1
  74.6 0.0 copy-done.2
  74.6 0.0 copy-done.3
  74.6 0.0 copy-start
  74.6 1.2 copy-done
  75.8 0.0 copy-start.4
  75.8 0.8 copy-done.4
  76.6 46.2 %merge_project_pool.1 = (bf16[256,512]{1,0:T(8,128)(2,1)S(1)}, f32[4,512]{1,0:T(4,128)S(1)}) custom-call(bf16[8,512,128]{2,1,0:T(8,128)(2,1)S(1)} %copy-done, f32[8,16,128]{2,1,0:T(8,128)S(1)} %copy-done.4, bf16[2,128,512]{2,1,0:T(8,128)(2,1)S(1)} %copy-done.3, s32[8,8,128]{2,1,0:T(8,128)S(1)} %copy-done.2, bf16[512,512]{1,0:T(8,128)(2,1)S(1)} %copy-done.1), custom_call_target="tpu_custom_call" | custom-call | tf_op jit(solution)/shard_map/merge_project_pool/pallas_call | solution.py:611
  122.9 0.7 copy.13
  123.6 0.6 copy.14
  (1 shorter events, 0.0 us)
Async XLA Ops:
  56.1 18.5 %copy-start.1 = (bf16[512,512]{1,0:T(8,128)(2,1)S(1)}, bf16[512,512]{1,0:T(8,128)(2,1)}, u32[]{:S(2)}) copy-start(bf16[512,512]{1,0:T(8,128)(2,1)} %w_out.1) | copy-start | bytes 1572868
  56.1 18.5 %copy-start.2 = (s32[8,8,128]{2,1,0:T(8,128)S(1)}, s32[8,8,128]{2,1,0:T(8,128)}, u32[]{:S(2)}) copy-start(s32[8,8,128]{2,1,0:T(8,128)} %get-tuple-element.11.lists.bits.ids) | copy-start | bytes 98308
  56.1 18.5 %copy-start.3 = (bf16[2,128,512]{2,1,0:T(8,128)(2,1)S(1)}, bf16[2,128,512]{2,1,0:T(8,128)(2,1)}, u32[]{:S(2)}) copy-start(bf16[2,128,512]{2,1,0:T(8,128)(2,1)} %get-tuple-element.19.dq) | copy-start | bytes 786436
  74.6 1.2 copy-start
  75.8 0.8 copy-start.4

commit v2 on v1

--- a/solution.py
+++ b/solution.py
@@ -14,7 +14,6 @@
 OUT_MASK = -3e38
 FLOOR = -1e30
 RING = 4
-NBUF = 4
 
 
 def place():
@@ -35,10 +34,10 @@
 
 
 def gather_kernel(
-    feat, wq, wk, wv, ints,
+    feat, wq_hbm, wk_hbm, wv_hbm, bits, slots, counts, ids,
     kb, vt, q_out, ints_out, dq_out, self_score, self_value,
-    fbuf, kk, vv, wqt, wkt, wvt, dq, got,
-    ring_send, ring_recv, sib_send, sib_recv, z_send, z_recv, i_send, i_recv, out_sem,
+    fbuf, wq, wk, wv, wqt, wkt, wvt, dq, ints, got,
+    ring_send, ring_recv, sib_send, sib_recv, z_send, z_recv, i_send, i_recv, in_sem,
 ):
     x, y, c, z = place()
     me = dst_index(x, y, c)
@@ -53,10 +52,22 @@
         for dc in range(2):
             if dy or dc:
                 peers.append((dst_index(x, y + dy, flip(c, dc)), z))
-    fbuf[me] = feat[...]
     barrier = pltpu.get_barrier_semaphore()
     for peer in peers:
         pl.semaphore_signal(barrier, inc=1, device_id=peer, device_id_type=MESH)
+    loads = [
+        pltpu.make_async_copy(src, dst, in_sem.at[n])
+        for n, (src, dst) in enumerate(((feat, fbuf.at[me]), (wv_hbm, wv), (wk_hbm, wk), (wq_hbm, wq)))
+    ]
+    for copy in loads:
+        copy.start()
+    for b in range(8):
+        ints[b] = jnp.zeros((8, BLK), I32)
+        ints[b, 0:1, :] = bits[b : b + 1, :]
+        ints[b, 1:2, 0:SLOTS] = slots[b]
+        ints[b, 2:3, :] = ids[b % 2 : b % 2 + 1, :]
+        ints[b, 3:4, :] = jnp.broadcast_to(counts[b : b + 1, :], (1, BLK))
+    loads[0].wait()
     pl.semaphore_wait(barrier, len(peers))
 
     def remote(src, dst, send, recv, to):
@@ -70,72 +81,63 @@
         copy.start()
         sent.append(copy)
 
-    def along(row, step):
-        if row == 0:
-            return (blk(c, step, 0), z)
-        return (blk(c, 0, step), z)
-
-    def full(row, i, step):
-        b = blk(c, i, 0)
-        s = 0 if step == 1 else 1
-        go(remote(fbuf.at[b], fbuf.at[b], ring_send.at[row, s], ring_recv.at[row, s], along(row, step)))
-
-    def fulls(row, i):
-        full(row, i, 1)
-        full(row, i, 3)
-
-    def half_ref(row, i, at, part):
-        b = blk(c, at, 0) if row == 0 else blk(c, i, at)
+    legs = ((3, 0, 1), (3, 1, 1), (1, 1, 3), (1, 0, 3), (2, 0, 1), (2, 1, 3))
+
+    def half_ref(row, at, part):
+        b = blk(c, at, 0) if row == 0 else blk(c, row - 1, at)
         return fbuf.at[b, pl.ds(part * BLK, BLK)]
 
-    def forward(row, i):
-        for part, frm, step in ((0, 3, 1), (1, 1, 3)):
-            r = half_ref(row, i, frm, part)
-            go(remote(r, r, ring_send.at[row, 2 + part], ring_recv.at[row, 2 + part], along(row, step)))
-
-    def wait_full(row, i):
-        for s, frm in ((0, 3), (1, 1)):
-            b = blk(c, frm, 0) if row == 0 else blk(c, i, frm)
-            remote(fbuf.at[b], fbuf.at[b], ring_send.at[row, s], ring_recv.at[row, s], (sibling, z)).wait_recv()
-
-    def wait_half(row, i):
-        for part in range(2):
-            r = half_ref(row, i, 2, part)
-            remote(r, r, ring_send.at[row, 2 + part], ring_recv.at[row, 2 + part], (sibling, z)).wait_recv()
-
-    def share(i, j):
-        b = blk(c, i, j)
-        go(remote(fbuf.at[b], fbuf.at[b], sib_send.at[i, j], sib_recv.at[i, j], (sibling, z)))
-
-    def wait_share(i, j):
-        b = blk(1 - c, i, j)
-        remote(fbuf.at[b], fbuf.at[b], sib_send.at[i, j], sib_recv.at[i, j], (sibling, z)).wait_recv()
-
-    def store(b, n):
-        return [
-            pltpu.make_async_copy(kk.at[b], kb.at[b], out_sem.at[b, 0]),
-            pltpu.make_async_copy(vv.at[b], vt.at[b], out_sem.at[b, 1]),
-        ]
+    def leg(row, n, at):
+        _, part, step = legs[n]
+        to = blk(c, step, 0) if row == 0 else blk(c, 0, step)
+        r = half_ref(row, at, part)
+        return remote(r, r, ring_send.at[row, n], ring_recv.at[row, n], (to, z))
+
+    def spread(row):
+        for n in (0, 2, 1, 3):
+            go(leg(row, n, 0))
+
+    def arrive(row, *ns):
+        for n in ns:
+            leg(row, n, legs[n][0]).wait_recv()
+
+    def forward(row):
+        arrive(row, 0)
+        go(leg(row, 4, 3))
+        arrive(row, 2)
+        go(leg(row, 5, 1))
+
+    def share(*places):
+        for i, j in places:
+            b = blk(c, i, j)
+            go(remote(fbuf.at[b], fbuf.at[b], sib_send.at[i, j], sib_recv.at[i, j], (sibling, z)))
+
+    def shared(*places):
+        for i, j in places:
+            b = blk(1 - c, i, j)
+            remote(fbuf.at[b], fbuf.at[b], sib_send.at[i, j], sib_recv.at[i, j], (sibling, z)).wait_recv()
 
     def project(b):
         f = fbuf[b]
-        kk[b] = jnp.dot(f, wk[...], preferred_element_type=F32).astype(BF)
+        kb[b] = jnp.dot(f, wk[...], preferred_element_type=F32).astype(BF)
         v = nt(wvt[...], f).astype(BF)
-        vv[b, 0] = v[:, :BLK]
-        vv[b, 1] = v[:, BLK:]
-        for copy in store(b, 0):
-            copy.start()
-
-    def project_many(n, where):
-        def body(e, carry):
-            project(where(e))
-            return carry
-
-        lax.fori_loop(0, n, body, 0)
-
-    fulls(0, 0)
-    fulls(1, 0)
-    share(0, 0)
+        vt[b, 0] = v[:, :BLK]
+        vt[b, 1] = v[:, BLK:]
+
+    def project_many(core, *places):
+        code = 0
+        for i, j in reversed(places):
+            code = code * 16 + 4 * i + j
+
+        def body(e, code):
+            project(blk(core, code % 16 // 4, code % 4))
+            return code // 16
+
+        lax.fori_loop(0, len(places), body, jnp.int32(code))
+
+    spread(0)
+    spread(1)
+    share((0, 0))
     for dy in range(4):
         for dc in range(2):
             s = (2 * y + dy) % 4
@@ -151,83 +153,63 @@
                         (dst_index(x, y + dy, flip(c, dc)), z),
                     )
                 )
+    for copy in loads[1:]:
+        copy.wait()
     wvt[...] = wv[...].T
     wqt[...] = wq[...].T
     wkt[...] = wk[...].T
+
+    forward(0)
+    forward(1)
     project(me)
-
-    wait_full(0, 0)
-    forward(0, 0)
-    fulls(4, 3)
-    fulls(2, 1)
-    share(3, 0)
-    share(1, 0)
-    wait_full(1, 0)
-    forward(1, 0)
-    share(0, 3)
-    share(0, 1)
-    project_many(4, lambda e: blk(c, (1 - e // 2) * (1 + 2 * e), (e // 2) * (2 * e - 3)))
-    wait_share(0, 0)
+    arrive(0, 1, 3)
+    spread(4)
+    spread(2)
+    share((3, 0), (1, 0))
+    arrive(1, 1, 3)
+    share((0, 3), (0, 1))
+    shared((0, 0))
     project(sibling)
-
-    wait_half(0, 0)
-    fulls(3, 2)
-    share(2, 0)
-    wait_half(1, 0)
-    share(0, 2)
-    project_many(2, lambda e: blk(c, 2 - 2 * e, 2 * e))
-    for i, j in ((1, 0), (3, 0), (0, 1), (0, 3)):
-        wait_share(i, j)
-    project_many(4, lambda e: blk(1 - c, (1 - e // 2) * (1 + 2 * e), (e // 2) * (2 * e - 3)))
-    wait_share(2, 0)
-    wait_share(0, 2)
+    arrive(0, 4, 5)
+    spread(3)
+    share((2, 0))
+    arrive(1, 4, 5)
+    share((0, 2))
+    project_many(c, (1, 0), (3, 0), (0, 1))
+    shared((1, 0), (3, 0), (0, 1), (0, 3), (2, 0), (0, 2))
 
     yy = (z - y + 4) % 4
 
     def plane_rows(cc):
         return fbuf.at[dst_index(x, yy, cc), pl.ds(pl.multiple_of(flip(c, cc) * BLK, BLK), BLK)]
 
-    for up, to in ((0, zup), (1, zdown)):
-        for cc in range(2):
+    for first in range(2):
+        for up, to in ((0, zup), (1, zdown)):
+            cc = flip(first, up)
             go(remote(plane_rows(cc), dq.at[z, cc], z_send.at[up, cc], z_recv.at[up, cc], (me, to)))
     own_copies = [pltpu.make_async_copy(plane_rows(cc), dq.at[z, cc], z_recv.at[3, cc]) for cc in range(2)]
     for copy in own_copies:
         copy.start()
 
-    wait_full(4, 3)
-    forward(4, 3)
-    share(3, 3)
-    share(3, 1)
-    wait_full(2, 1)
-    forward(2, 1)
-    share(1, 3)
-    share(1, 1)
-    project_many(4, lambda e: blk(c, 1 + 2 * (e // 2), 1 + 2 * (e % 2)))
-    project_many(2, lambda e: blk(1 - c, 2 - 2 * e, 2 * e))
-
-    wait_half(4, 3)
-    share(3, 2)
-    wait_half(2, 1)
-    share(1, 2)
-    for up, frm in ((0, zdown), (1, zup)):
-        for cc in range(2):
-            remote(dq.at[frm, cc], dq.at[frm, cc], z_send.at[up, cc], z_recv.at[up, cc], (me, zup)).wait_recv()
-    for cc, frm, to in ((0, zdown, zup), (1, zup, zdown)):
-        go(remote(dq.at[frm, cc], dq.at[frm, cc], z_send.at[2, cc], z_recv.at[2, cc], (me, to)))
-    project_many(2, lambda e: blk(c, 1 + 2 * e, 2))
-    for i in (1, 3):
-        for j in (1, 3):
-            wait_share(i, j)
-    project_many(4, lambda e: blk(1 - c, 1 + 2 * (e // 2), 1 + 2 * (e % 2)))
-
-    wait_full(3, 2)
-    forward(3, 2)
-    share(2, 3)
-    share(2, 1)
-    project_many(2, lambda e: blk(c, 2, 1 + 2 * e))
-    wait_share(1, 2)
-    wait_share(3, 2)
-    project_many(2, lambda e: blk(1 - c, 1 + 2 * e, 2))
+    forward(4)
+    forward(2)
+    project_many(c, (0, 3), (2, 0), (0, 2))
+    arrive(4, 1, 3)
+    share((3, 3), (3, 1))
+    arrive(2, 1, 3)
+    share((1, 3), (1, 1))
+    project_many(1 - c, (1, 0), (3, 0))
+    forward(3)
+
+    def z_leg(up, cc, frm):
+        return remote(dq.at[frm, cc], dq.at[frm, cc], z_send.at[up, cc], z_recv.at[up, cc], (me, zup))
+
+    z_leg(0, 0, zdown).wait_recv()
+    go(remote(dq.at[zdown, 0], dq.at[zdown, 0], z_send.at[2, 0], z_recv.at[2, 0], (me, zup)))
+    z_leg(1, 1, zup).wait_recv()
+    go(remote(dq.at[zup, 1], dq.at[zup, 1], z_send.at[2, 1], z_recv.at[2, 1], (me, zdown)))
+    project_many(1 - c, (0, 1), (0, 3), (2, 0), (0, 2))
+    project_many(c, (1, 1), (1, 3), (3, 1), (3, 3))
     for copy in own_copies:
         copy.wait()
 
@@ -239,6 +221,14 @@
         query((z + 3 + e // 2) % 4, e % 2)
         return carry
 
+    z_leg(0, 1, zdown).wait_recv()
+    z_leg(1, 0, zup).wait_recv()
+    arrive(4, 4, 5)
+    share((3, 2))
+    arrive(2, 4, 5)
+    share((1, 2))
+    shared((1, 1), (1, 3), (3, 1), (3, 3))
+    project_many(1 - c, (1, 1), (1, 3), (3, 1), (3, 3))
     lax.fori_loop(0, 6, queries, 0)
     for cc in range(2):
         f = dq[z, cc]
@@ -259,74 +249,65 @@
                     got.at[slot], got.at[slot], i_send.at[dy, dc], i_recv.at[dy, dc], (sibling, z)
                 ).wait_recv()
     ints_out[...] = got[...]
-
-    wait_half(3, 2)
-    share(2, 2)
-    project(blk(c, 2, 2))
-    wait_share(2, 1)
-    wait_share(2, 3)
-    project_many(2, lambda e: blk(1 - c, 2, 1 + 2 * e))
+    project_many(c, (1, 2), (3, 2))
+    arrive(3, 1, 3)
+    share((2, 3), (2, 1))
     far = (z + 2) % 4
     for cc in range(2):
-        remote(dq.at[far, cc], dq.at[far, cc], z_send.at[2, cc], z_recv.at[2, cc], (me, zup)).wait_recv()
+        z_leg(2, cc, far).wait_recv()
     for cc in range(2):
         query(far, cc)
-    wait_share(2, 2)
-    project(blk(1 - c, 2, 2))
-
-    def drain(b, carry):
-        for copy in store(b, 0):
-            copy.wait()
-        return carry
-
-    lax.fori_loop(0, 32, drain, 0)
+    shared((1, 2), (3, 2))
+    project_many(1 - c, (1, 2), (3, 2))
+    project_many(c, (2, 1), (2, 3))
+    arrive(3, 4, 5)
+    share((2, 2))
+    project_many(c, (2, 2))
+    shared((2, 1), (2, 3), (2, 2))
+    project_many(1 - c, (2, 1), (2, 3), (2, 2))
     for copy in sent:
         copy.wait_send()
 
 
-def gather_call(feat, wq, wk, wv, ints):
+def gather_call(*args):
+    hbm = pl.BlockSpec(memory_space=pltpu.HBM)
     vm = pl.BlockSpec(memory_space=pltpu.VMEM)
-    anyw = pl.BlockSpec(memory_space=pl.ANY)
     dma = pltpu.SemaphoreType.DMA
     return pl.pallas_call(
         gather_kernel,
         out_shape=(
-            jax.ShapeDtypeStruct((32, ROWS, WIDTH), BF),
-            jax.ShapeDtypeStruct((32, 2, WIDTH, BLK), BF),
-            jax.ShapeDtypeStruct((8, WIDTH, BLK), BF),
+            pltpu.VMEM((32, ROWS, WIDTH), BF),
+            pltpu.VMEM((32, 2, WIDTH, BLK), BF),
+            pltpu.VMEM((8, WIDTH, BLK), BF),
             jax.ShapeDtypeStruct((8, 8, BLK), I32),
-            jax.ShapeDtypeStruct((2, BLK, WIDTH), BF),
-            jax.ShapeDtypeStruct((2, HEADS, BLK), F32),
-            jax.ShapeDtypeStruct((2, WIDTH, BLK), BF),
+            pltpu.VMEM((2, BLK, WIDTH), BF),
+            pltpu.VMEM((2, HEADS, BLK), F32),
+            pltpu.VMEM((2, WIDTH, BLK), BF),
         ),
-        in_specs=[vm] * 5,
-        out_specs=(anyw, anyw, vm, vm, vm, vm, vm),
+        in_specs=[hbm] * 4 + [vm] * 4,
+        out_specs=(vm,) * 7,
         scratch_shapes=[
             pltpu.VMEM((32, ROWS, WIDTH), BF),
-            pltpu.VMEM((32, ROWS, WIDTH), BF),
-            pltpu.VMEM((32, 2, WIDTH, BLK), BF),
-            pltpu.VMEM((WIDTH, WIDTH), BF),
-            pltpu.VMEM((WIDTH, WIDTH), BF),
-            pltpu.VMEM((WIDTH, WIDTH), BF),
+            *[pltpu.VMEM((WIDTH, WIDTH), BF)] * 6,
             pltpu.VMEM((4, 2, BLK, WIDTH), BF),
             pltpu.VMEM((8, 8, BLK), I32),
-            dma((5, 4)), dma((5, 4)), dma((4, 4)), dma((4, 4)),
-            dma((3, 2)), dma((4, 2)), dma((4, 2)), dma((4, 2)), dma((32, 2)),
+            pltpu.VMEM((8, 8, BLK), I32),
+            dma((5, 6)), dma((5, 6)), dma((4, 4)), dma((4, 4)),
+            dma((3, 2)), dma((4, 2)), dma((4, 2)), dma((4, 2)), dma((4,)),
         ],
         compiler_params=pltpu.CompilerParams(
-            collective_id=0, has_side_effects=True, vmem_limit_bytes=56 << 20
+            collective_id=0, has_side_effects=True, vmem_limit_bytes=44 << 20
         ),
         name="gather_project",
-    )(feat, wq, wk, wv, ints)
+    )(*args)
 
 
 def attention_kernel(
-    lists, where_ref, qt, bits, self_score, self_value, kb, vt,
+    lists, qt, bits, self_score, self_value, kb, vt,
     acc_out, stat_out,
-    et, rhs, acc, m, l, kbuf, vbuf, sem, sched, sx, sy,
+    et, rhs, acc, m, l, sched, sx, sy, mx, my,
 ):
-    z = where_ref[0]
-    base = where_ref[1]
+    x, y, c, z = place()
     lane = lax.broadcasted_iota(I32, (BLK, BLK), 1)
     row = lax.broadcasted_iota(I32, (BLK, BLK), 0)
     for ph in range(15):
@@ -337,7 +318,7 @@
         return (4 * ((g // 2) * 8 + 2 * z + g % 2)) % 15
 
     def build(b, n):
-        count = lists[b, 1, SLOTS]
+        count = lists[b, 3, 0]
 
         def inner(t, n):
             first = lists[b, 1, 2 * t]
@@ -357,23 +338,6 @@
         for f in range(5):
             sched[f, steps + extra] = 15 if f >= 3 else 0
     even = 2 * ((steps + 1) // 2)
-
-    def copies(i):
-        slot = lax.rem(i, NBUF)
-        a, b = sched[1, i], sched[2, i]
-        return [
-            pltpu.make_async_copy(kb.at[a], kbuf.at[slot, 0], sem.at[slot, 0]),
-            pltpu.make_async_copy(kb.at[b], kbuf.at[slot, 1], sem.at[slot, 1]),
-            pltpu.make_async_copy(vt.at[a], vbuf.at[slot, 0], sem.at[slot, 2]),
-            pltpu.make_async_copy(vt.at[b], vbuf.at[slot, 1], sem.at[slot, 3]),
-        ]
-
-    for i in range(NBUF - 1):
-
-        @pl.when(i <= even)
-        def _():
-            for copy in copies(i):
-                copy.start()
 
     def prepare(b, carry):
         brow = bits[b, 0:1, :]
@@ -398,7 +362,7 @@
     lax.fori_loop(0, 8, prepare, 0)
     for cc in range(2):
         b = 2 * z + cc
-        start = where_ref[2 + cc] * BLK
+        start = (dst_index(x, z - y + 4, cc) * 8 + 2 * z + flip(c, cc)) * BLK
         lanes = lax.broadcasted_iota(I32, (1, BLK), 1)
         on = (bits[b, 0:1, :] >> ((start + lanes) % 30)) & 1
         extra = jnp.broadcast_to(on, (HEADS, BLK)) == 0
@@ -408,52 +372,43 @@
             jnp.broadcast_to(on, (WIDTH, BLK)) == 0, self_value[cc].astype(F32), 0.0
         )
 
-    def scores(i, out, p):
-        slot = lax.rem(i, NBUF)
+    def scores(i, out, tops, p):
         e0, e1, b = et[sched[3, i]], et[sched[4, i]], sched[0, i]
-        k0 = kbuf[slot, 0, :, 128 * p : 128 * p + 128]
-        k1 = kbuf[slot, 1, :, 128 * p : 128 * p + 128]
+        cols = slice(128 * p, 128 * p + 128)
+        k0, k1 = kb[sched[1, i], :, cols], kb[sched[2, i], :, cols]
         lhs = jnp.concatenate([jnp.concatenate([k0, e0], 1), jnp.concatenate([k1, e1], 1)], 0)
-        out[p] = jnp.dot(lhs, rhs[b, p], preferred_element_type=F32)
-
-    def head(i, cur, h):
-        slot, b = lax.rem(i, NBUF), sched[0, i]
+        s = jnp.dot(lhs, rhs[b, p], preferred_element_type=F32)
+        out[p] = s
+        top = jnp.max(s.reshape(32, 8, 256), axis=0)
+        tops[2 * p] = top[:, :128]
+        tops[2 * p + 1] = top[:, 128:]
+
+    def head(i, cur, tops, h):
+        b = sched[0, i]
         p, side = h // 2, h % 2
         old = m[b, h : h + 1, :]
-        s = cur[p, :, 128 * side : 128 * side + 128]
-        top = jnp.maximum(old, jnp.max(s, axis=0, keepdims=True))
+        top = jnp.maximum(old, jnp.max(tops[h], axis=0, keepdims=True))
         factor = jnp.exp(old - top)
         w = jnp.exp(cur[p, :, 128 * side : 128 * side + 128] - top)
         m[b, h : h + 1, :] = top
         l[b, h : h + 1, :] = l[b, h : h + 1, :] * factor + jnp.sum(w, axis=0, keepdims=True)
         rows = slice(64 * h, 64 * h + 64)
-        v = jnp.concatenate([vbuf[slot, 0, rows, :], vbuf[slot, 1, rows, :]], 1)
+        v = jnp.concatenate([vt[sched[1, i], rows, :], vt[sched[2, i], rows, :]], 1)
         o = jnp.dot(v, w.astype(BF), preferred_element_type=F32)
         acc[b, rows, :] = acc[b, rows, :] * factor + o
 
-    def wait(i):
-        for copy in copies(i):
-            copy.wait()
-
-    def step(i, cur, nxt):
-        @pl.when(i + NBUF - 1 <= even)
-        def _():
-            for copy in copies(i + NBUF - 1):
-                copy.start()
-
-        wait(i + 1)
+    def step(i, cur, tops, nxt, next_tops):
         for p in range(4):
-            scores(i + 1, nxt, p)
-            head(i, cur, 2 * p)
-            head(i, cur, 2 * p + 1)
-
-    wait(0)
+            scores(i + 1, nxt, next_tops, p)
+            head(i, cur, tops, 2 * p)
+            head(i, cur, tops, 2 * p + 1)
+
     for p in range(4):
-        scores(0, sx, p)
+        scores(0, sx, mx, p)
 
     def body(j, carry):
-        step(2 * j, sx, sy)
-        step(2 * j + 1, sy, sx)
+        step(2 * j, sx, mx, sy, my)
+        step(2 * j + 1, sy, my, sx, mx)
         return carry
 
     lax.fori_loop(0, even // 2, body, 0)
@@ -462,17 +417,16 @@
     stat_out[:, 8:16, :] = l[...]
 
 
-def attention_call(ints, where, qt, self_score, self_value, kb, vt):
+def attention_call(ints, qt, self_score, self_value, kb, vt):
     vm = pl.BlockSpec(memory_space=pltpu.VMEM)
     sm = pl.BlockSpec(memory_space=pltpu.SMEM)
-    anyw = pl.BlockSpec(memory_space=pl.ANY)
     return pl.pallas_call(
         attention_kernel,
         out_shape=(
-            jax.ShapeDtypeStruct((8, WIDTH, BLK), BF),
-            jax.ShapeDtypeStruct((8, 16, BLK), F32),
+            pltpu.VMEM((8, WIDTH, BLK), BF),
+            pltpu.VMEM((8, 16, BLK), F32),
         ),
-        in_specs=[sm, sm, vm, vm, vm, vm, anyw, anyw],
+        in_specs=[sm, vm, vm, vm, vm, vm, vm],
         out_specs=(vm, vm),
         scratch_shapes=[
             pltpu.VMEM((16, BLK, BLK), BF),
@@ -480,16 +434,15 @@
             pltpu.VMEM((8, WIDTH, BLK), F32),
             pltpu.VMEM((8, HEADS, BLK), F32),
             pltpu.VMEM((8, HEADS, BLK), F32),
-            pltpu.VMEM((NBUF, 2, BLK, WIDTH), BF),
-            pltpu.VMEM((NBUF, 2, WIDTH, BLK), BF),
-            pltpu.SemaphoreType.DMA((NBUF, 4)),
             pltpu.SMEM((5, 136), I32),
             pltpu.VMEM((4, 256, 256), F32),
             pltpu.VMEM((4, 256, 256), F32),
+            pltpu.VMEM((8, 8, BLK), F32),
+            pltpu.VMEM((8, 8, BLK), F32),
         ],
-        compiler_params=pltpu.CompilerParams(vmem_limit_bytes=56 << 20),
+        compiler_params=pltpu.CompilerParams(vmem_limit_bytes=24 << 20),
         name="block_attention",
-    )(ints, where, qt, ints, self_score, self_value, kb, vt)
+    )(ints, qt, ints, self_score, self_value, kb, vt)
 
 
 def merge_kernel(
@@ -629,26 +582,19 @@
             dma((8,)), dma((8,)), dma((16,)), dma((16,)),
         ],
         compiler_params=pltpu.CompilerParams(
-            collective_id=1, has_side_effects=True, vmem_limit_bytes=40 << 20
+            collective_id=1, has_side_effects=True, vmem_limit_bytes=16 << 20
         ),
         name="merge_project_pool",
     )(acc, stat, dq, ids, w_out)
 
 
 def shards(features, w_query, w_key, w_value, w_out, node_bits, block_src, block_count, graph_ids):
-    x, y, c, z = place()
-    bits = node_bits.reshape(8, 1, BLK)
-    slots = jnp.concatenate(
-        [block_src, jnp.broadcast_to(block_count[:, :, None], (8, 1, BLK - SLOTS))], axis=2
+    kb, vt, qt, got, dq, self_score, self_value = gather_call(
+        features, w_query, w_key, w_value,
+        node_bits.reshape(8, BLK), block_src, block_count, graph_ids.reshape(2, BLK),
     )
-    ids = jnp.tile(graph_ids.reshape(2, 1, BLK), (4, 1, 1))
-    ints = jnp.concatenate([bits, slots, ids, jnp.zeros((8, 5, BLK), I32)], axis=1)
-    kb, vt, qt, got, dq, self_score, self_value = gather_call(features, w_query, w_key, w_value, ints)
-    yy = (z - y + 4) % 4
-    own = [dst_index(x, yy, cc) * 8 + 2 * z + flip(c, cc) for cc in range(2)]
-    where = jnp.stack([z, z, own[0], own[1]]).astype(I32)
     acc, stat = attention_call(
-        got, where, qt, self_score, self_value, kb.reshape(64, BLK, WIDTH), vt.reshape(64, WIDTH, BLK)
+        got, qt, self_score, self_value, kb.reshape(64, BLK, WIDTH), vt.reshape(64, WIDTH, BLK)
     )
     return merge_call(acc, stat, dq, got, w_out)
 

time: 125 us -> 111 us (0.89)
  Pallas kernels: 116 us -> 106 us
  other arithmetic: 2.07 us -> 0 us
  local copies, waits for them, and re-layouts: 4.86 us -> 3.38 us
    pallas_call x2, Pallas kernels: 70.2 us -> 62.9 us  [the longest x1 43.6 us: gather_call(): pl.pallas_call(gather_kernel, out_shape=(pltpu.VMEM((32, ROWS, WIDTH), BF...]
    pallas_call x1, Pallas kernels: 46.2 us -> 43.5 us  [merge_call(): pl.pallas_call(merge_kernel, out_shape=(jax.ShapeDtypeStruct((ROWS, WIDTH...]
    concatenate x1 -> x0, other arithmetic: 1.4 us -> none  [shards(): jnp.concatenate([bits, slots, ids, jnp.zeros((8, 5, BLK), I32)], axis=1)]
    unnamed x12 -> x7, local copies, waits for them, and re-layouts: 3.37 us -> 3.38 us
where the time goes in v2:
time: 111 us; the launch traced here: 110 us
  Pallas kernels  106 us (95%)
  local copies, waits for them, and re-layouts  3.38 us (3%)
    pallas_call x1, Pallas kernels, gather_call(): pl.pallas_call(gather_kernel, out_shape=(pltpu.VMEM((32, ROWS, WIDTH), BF...  43.6 us
    pallas_call x1, Pallas kernels, merge_call(): pl.pallas_call(merge_kernel, out_shape=(jax.ShapeDtypeStruct((ROWS, WIDTH...  43.5 us
    pallas_call x1, Pallas kernels, attention_call(): pl.pallas_call(attention_kernel, out_shape=(pltpu.VMEM((8, WIDTH, BLK), B...  19.3 us
    unnamed x7, local copies, waits for them, and re-layouts  3.38 us

profile of v2, /device:TPU:1, one launch (start us, length us, event | category | flops | bytes accessed | tf_op | source)
XLA Modules:
  0.0 110.4 jit_solution(13075627226943477486)
XLA Ops:
  0.6 1.3 %copy.11.counts = s32[8,1]{1,0:T(8,128)} copy(s32[8,1]{0,1:T(1,128)} %param.16) | data formatting | bytes 64 | tf_op args[7]
  2.0 43.6 %gather_project.1 = (bf16[32,256,512]{2,1,0:T(8,128)(2,1)S(1)}, bf16[32,2,512,128]{3,2,1,0:T(8,128)(2,1)S(1)}, bf16[8,512,128]{2,1,0:T(8,128)(2,1)S(1)}, s32[8,8...) custom-call(bf16[256,512]{1,0:T(8,128)(2,1)} %feat.1, ...), custom_call_target="tpu_custom_call" | custom-call | tf_op jit(solution)/shard_map/gather_project/pallas_call | solution.py:276
  45.5 0.0 copy-start.1
  45.5 0.7 copy-done.1
  46.3 0.0 copy-start
  46.3 19.3 %block_attention.1 = (bf16[8,512,128]{2,1,0:T(8,128)(2,1)S(1)}, f32[8,16,128]{2,1,0:T(8,128)S(1)}) custom-call(s32[8,8,128]{2,1,0:T(8,128)S(1)} %copy-done.1, bf16[8,512,128]{2,1,0:T(8,128)(2,1)S(1)} %get-tuple-element.12.qt, s32[8,8,128]{2,1,0:T(8,128)S(1)} %copy-done.1, f32[2,8,128]{2,1,0:T(8,128)S(1)} %get-tuple-element.13.self_score, ...), custom_call_target="tpu_custom_call" | custom-call | tf_op jit(solution)/shard_map/block_attention/pallas_call | solution.py:423
  65.6 0.0 copy-done
  65.6 43.5 %merge_project_pool.1 = (bf16[256,512]{1,0:T(8,128)(2,1)S(1)}, f32[4,512]{1,0:T(4,128)S(1)}) custom-call(bf16[8,512,128]{2,1,0:T(8,128)(2,1)S(1)} %get-tuple-element.17.acc, f32[8,16,128]{2,1,0:T(8,128)S(1)} %get-tuple-element.18.stat, bf16[2,128,512]{2,1,0:T(8,128)(2,1)S(1)} %get-tuple-element.19.dq, s32[8,8,128]{2,1,0:T(8,128)S(1)} %copy-done.1, ...), custom_call_target="tpu_custom_call" | custom-call | tf_op jit(solution)/shard_map/merge_project_pool/pallas_call | solution.py:564
  109.1 0.7 copy.14
  109.8 0.6 copy.15
Async XLA Ops:
  45.5 0.8 copy-start.1
  46.3 19.3 %copy-start = (bf16[512,512]{1,0:T(8,128)(2,1)S(1)}, bf16[512,512]{1,0:T(8,128)(2,1)}, u32[]{:S(2)}) copy-start(bf16[512,512]{1,0:T(8,128)(2,1)} %w_out.1) | copy-start | bytes 1572868

commit v3 on v2

--- a/solution.py
+++ b/solution.py
@@ -153,28 +153,25 @@
                         (dst_index(x, y + dy, flip(c, dc)), z),
                     )
                 )
+    forward(0)
+    forward(1)
     for copy in loads[1:]:
         copy.wait()
     wvt[...] = wv[...].T
-    wqt[...] = wq[...].T
-    wkt[...] = wk[...].T
-
-    forward(0)
-    forward(1)
-    project(me)
     arrive(0, 1, 3)
     spread(4)
     spread(2)
     share((3, 0), (1, 0))
-    arrive(1, 1, 3)
-    share((0, 3), (0, 1))
-    shared((0, 0))
-    project(sibling)
     arrive(0, 4, 5)
     spread(3)
     share((2, 0))
+    arrive(1, 1, 3)
+    share((0, 3), (0, 1))
     arrive(1, 4, 5)
     share((0, 2))
+    shared((0, 0))
+    project(me)
+    project(sibling)
     project_many(c, (1, 0), (3, 0), (0, 1))
     shared((1, 0), (3, 0), (0, 1), (0, 3), (2, 0), (0, 2))
 
@@ -194,6 +191,8 @@
     forward(4)
     forward(2)
     project_many(c, (0, 3), (2, 0), (0, 2))
+    wqt[...] = wq[...].T
+    wkt[...] = wk[...].T
     arrive(4, 1, 3)
     share((3, 3), (3, 1))
     arrive(2, 1, 3)
@@ -448,7 +447,7 @@
 def merge_kernel(
     acc, stat, dq, ids, w_out,
     updated_out, pooled_out,
-    acc_got, stat_got, made, mine, part, ring_part, total, all_part,
+    acc_got, stat_got, acc_way, stat_way, made, mine, part, ring_part, total, all_part,
     a_send, a_recv, s_send, s_recv, u_send, u_recv, r_send, r_recv, g_send, g_recv,
 ):
     x, y, c, z = place()
@@ -479,44 +478,70 @@
         copy.start()
         sent.append(copy)
 
-    for dz in (2, 1, 3):
-        to = (z + dz) % 4
-        rows = pl.ds(2 * to, 2)
-        go(remote(acc.at[rows], acc_got.at[dz - 1], a_send.at[dz - 1], a_recv.at[dz - 1], (me, to)))
-        go(remote(stat.at[rows], stat_got.at[dz - 1], s_send.at[dz - 1], s_recv.at[dz - 1], (me, to)))
-    for dz in (1, 3, 2):
-        rows = pl.ds(2 * z, 2)
-        remote(acc.at[rows], acc_got.at[dz - 1], a_send.at[dz - 1], a_recv.at[dz - 1], (me, z)).wait_recv()
-        remote(stat.at[rows], stat_got.at[dz - 1], s_send.at[dz - 1], s_recv.at[dz - 1], (me, z)).wait_recv()
-    yy = (z - y + 4) % 4
-    for cc in range(2):
-        b = 2 * z + cc
-        stats = [stat[b]] + [stat_got[k, cc] for k in range(3)]
+    zup, zdown, zfar = (z + 1) % 4, (z + 3) % 4, (z + 2) % 4
+
+    def ship(slot, acc_ref, stat_ref, to):
+        go(remote(acc_ref, acc_got.at[slot], a_send.at[slot], a_recv.at[slot], (me, to)))
+        go(remote(stat_ref, stat_got.at[slot], s_send.at[slot], s_recv.at[slot], (me, to)))
+
+    def landed(slot):
+        remote(acc.at[0], acc_got.at[slot], a_send.at[slot], a_recv.at[slot], (me, zup)).wait_recv()
+        remote(stat.at[0], stat_got.at[slot], s_send.at[slot], s_recv.at[slot], (me, zup)).wait_recv()
+
+    for side, to in ((0, zup), (1, zdown)):
+        ship(side, acc.at[2 * zfar + side], stat.at[2 * zfar + side], to)
+    for side, to in ((0, zup), (1, zdown)):
+        b = 2 * to + 1 - side
+        ship(2 + side, acc.at[b], stat.at[b], to)
+
+    def weigh(stats):
         top = stats[0][0:8]
         for s in stats[1:]:
             top = jnp.maximum(top, s[0:8])
         factors = [jnp.exp(s[0:8] - top) for s in stats]
-        whole = sum(f * s[8:16] for f, s in zip(factors, stats))
+        return top, factors, sum(f * s[8:16] for f, s in zip(factors, stats))
+
+    for side, to in ((0, zup), (1, zdown)):
+        b = 2 * to + side
+        landed(side)
+        top, factors, whole = weigh([stat[b], stat_got[side]])
+        stat_way[side, 0:8] = top
+        stat_way[side, 8:16] = whole
+        for h in range(HEADS):
+            rows = slice(64 * h, 64 * h + 64)
+            acc_way[side, rows] = (
+                acc[b, rows, :].astype(F32) * factors[0][h : h + 1, :]
+                + acc_got[side, rows, :].astype(F32) * factors[1][h : h + 1, :]
+            ).astype(BF)
+        ship(4 + side, acc_way.at[side], stat_way.at[side], to)
+    for side in range(2):
+        landed(2 + side)
+    yy = (z - y + 4) % 4
+    for cc in range(2):
+        b = 2 * z + cc
+        landed(4 + cc)
+        slots = (3 - cc, 4 + cc)
+        _, factors, whole = weigh([stat[b]] + [stat_got[k] for k in slots])
         inv = 1.0 / whole
         factors = [f * inv for f in factors]
         pieces = []
         for h in range(HEADS):
             rows = slice(64 * h, 64 * h + 64)
             o = acc[b, rows, :].astype(F32) * factors[0][h : h + 1, :]
-            for k in range(3):
-                o = o + acc_got[k, cc, rows, :].astype(F32) * factors[k + 1][h : h + 1, :]
+            for n, k in enumerate(slots):
+                o = o + acc_got[k, rows, :].astype(F32) * factors[n + 1][h : h + 1, :]
             pieces.append(o)
         att = jnp.concatenate(pieces, 0).T.astype(BF)
         mixed = jnp.dot(att, w_out[...], preferred_element_type=F32)
         new = (dq[cc].astype(F32) + mixed).astype(BF)
         made[cc] = new
         gid = ids[b, 2:3, :]
-        member = jnp.where(
-            jnp.broadcast_to(gid, (8, BLK)) == lax.broadcasted_iota(I32, (8, BLK), 0), 1.0, 0.0
-        )
+        graph = lax.broadcasted_iota(I32, (8, BLK), 0) % 4
+        member = jnp.where(jnp.broadcast_to(gid, (8, BLK)) == graph, 1.0, 0.0)
         sums = jnp.dot(member.astype(BF), new, preferred_element_type=F32)
+        low = lax.broadcasted_iota(I32, (8, 256), 0) < 4
         counts = jnp.broadcast_to(jnp.sum(member, axis=1, keepdims=True), (8, BLK))
-        both = jnp.concatenate([sums, counts], 1)
+        both = jnp.concatenate([jnp.where(low, sums[:, :256], sums[:, 256:]), counts], 1)
         part[...] = both if cc == 0 else part[...] + both
     for cc in range(2):
         own = jnp.logical_and(yy == y, c == cc)
@@ -545,8 +570,9 @@
         k = 4 * dx + dz
         remote(total, all_part.at[k], g_send.at[k], g_recv.at[k], to).wait_recv()
         whole = whole + all_part[k]
-    scale = 1.0 / jnp.sqrt(jnp.concatenate([whole[0:4, WIDTH:]] * 4, 1))
-    pooled_out[...] = whole[0:4, :WIDTH] * scale
+    scale = 1.0 / jnp.sqrt(jnp.concatenate([whole[0:4, 256:]] * 2, 1))
+    pooled_out[:, 0:256] = whole[0:4, 0:256] * scale
+    pooled_out[:, 256:512] = whole[4:8, 0:256] * scale
     for cc in range(2):
         own = jnp.logical_and(yy == y, c == cc)
         copy = remote(
@@ -570,15 +596,17 @@
         in_specs=[vm] * 5,
         out_specs=(vm, vm),
         scratch_shapes=[
-            pltpu.VMEM((3, 2, WIDTH, BLK), BF),
-            pltpu.VMEM((3, 2, 16, BLK), F32),
+            pltpu.VMEM((6, WIDTH, BLK), BF),
+            pltpu.VMEM((6, 16, BLK), F32),
+            pltpu.VMEM((2, WIDTH, BLK), BF),
+            pltpu.VMEM((2, 16, BLK), F32),
             pltpu.VMEM((2, BLK, WIDTH), BF),
             pltpu.VMEM((2, BLK, WIDTH), BF),
-            pltpu.VMEM((8, WIDTH + BLK), F32),
-            pltpu.VMEM((8, 8, WIDTH + BLK), F32),
-            pltpu.VMEM((8, WIDTH + BLK), F32),
-            pltpu.VMEM((16, 8, WIDTH + BLK), F32),
-            dma((3,)), dma((3,)), dma((3,)), dma((3,)), dma((2,)), dma((2,)),
+            pltpu.VMEM((8, 256 + BLK), F32),
+            pltpu.VMEM((8, 8, 256 + BLK), F32),
+            pltpu.VMEM((8, 256 + BLK), F32),
+            pltpu.VMEM((16, 8, 256 + BLK), F32),
+            dma((6,)), dma((6,)), dma((6,)), dma((6,)), dma((2,)), dma((2,)),
             dma((8,)), dma((8,)), dma((16,)), dma((16,)),
         ],
         compiler_params=pltpu.CompilerParams(

time: 111 us -> 109 us (0.982)
    pallas_call x1, Pallas kernels: 19.3 us -> 13.5 us  [attention_call(): pl.pallas_call(attention_kernel, out_shape=(pltpu.VMEM((8, WIDTH, BLK), B...]
    pallas_call x1, Pallas kernels: 43.5 us -> 47.4 us  [merge_call(): pl.pallas_call(merge_kernel, out_shape=(jax.ShapeDtypeStruct((ROWS, WIDTH...]
where the time goes in v3:
time: 109 us
  Pallas kernels  105 us (96%)
  local copies, waits for them, and re-layouts  3.38 us (3%)
    pallas_call x1, Pallas kernels, merge_call(): pl.pallas_call(merge_kernel, out_shape=(jax.ShapeDtypeStruct((ROWS, WIDTH...  47.4 us
    pallas_call x1, Pallas kernels, gather_call(): pl.pallas_call(gather_kernel, out_shape=(pltpu.VMEM((32, ROWS, WIDTH), BF...  43.7 us
    pallas_call x1, Pallas kernels, attention_call(): pl.pallas_call(attention_kernel, out_shape=(pltpu.VMEM((8, WIDTH, BLK), B...  13.5 us
    unnamed x7, local copies, waits for them, and re-layouts  3.38 us

profile of v3, /device:TPU:1, one launch (start us, length us, event | category | flops | bytes accessed | tf_op | source)
XLA Modules:
  0.0 108.6 jit_solution(2888749055167315455)
XLA Ops:
  0.6 1.3 %copy.11.counts = s32[8,1]{1,0:T(8,128)} copy(s32[8,1]{0,1:T(1,128)} %param.16) | data formatting | bytes 64 | tf_op args[7]
  2.0 43.7 %gather_project.1 = (bf16[32,256,512]{2,1,0:T(8,128)(2,1)S(1)}, bf16[32,2,512,128]{3,2,1,0:T(8,128)(2,1)S(1)}, bf16[8,512,128]{2,1,0:T(8,128)(2,1)S(1)}, s32[8,8...) custom-call(bf16[256,512]{1,0:T(8,128)(2,1)} %feat.1, ...), custom_call_target="tpu_custom_call" | custom-call | tf_op jit(solution)/shard_map/gather_project/pallas_call | solution.py:275
  45.6 0.0 copy-start.1
  45.6 0.7 copy-done.1
  46.4 0.0 copy-start
  46.4 13.5 %block_attention.1 = (bf16[8,512,128]{2,1,0:T(8,128)(2,1)S(1)}, f32[8,16,128]{2,1,0:T(8,128)S(1)}) custom-call(s32[8,8,128]{2,1,0:T(8,128)S(1)} %copy-done.1, bf16[8,512,128]{2,1,0:T(8,128)(2,1)S(1)} %get-tuple-element.12.qt, s32[8,8,128]{2,1,0:T(8,128)S(1)} %copy-done.1, f32[2,8,128]{2,1,0:T(8,128)S(1)} %get-tuple-element.13.self_score, ...), custom_call_target="tpu_custom_call" | custom-call | tf_op jit(solution)/shard_map/block_attention/pallas_call | solution.py:422
  59.9 0.0 copy-done
  59.9 47.4 %merge_project_pool.1 = (bf16[256,512]{1,0:T(8,128)(2,1)S(1)}, f32[4,512]{1,0:T(4,128)S(1)}) custom-call(bf16[8,512,128]{2,1,0:T(8,128)(2,1)S(1)} %get-tuple-element.17.acc, f32[8,16,128]{2,1,0:T(8,128)S(1)} %get-tuple-element.18.stat, bf16[2,128,512]{2,1,0:T(8,128)(2,1)S(1)} %get-tuple-element.19.dq, s32[8,8,128]{2,1,0:T(8,128)S(1)} %copy-done.1, ...), custom_call_target="tpu_custom_call" | custom-call | tf_op jit(solution)/shard_map/merge_project_pool/pallas_call | solution.py:590
  107.3 0.7 copy.14
  108.0 0.6 copy.15
Async XLA Ops:
  45.6 0.8 copy-start.1
  46.4 13.5 %copy-start = (bf16[512,512]{1,0:T(8,128)(2,1)S(1)}, bf16[512,512]{1,0:T(8,128)(2,1)}, u32[]{:S(2)}) copy-start(bf16[512,512]{1,0:T(8,128)(2,1)} %w_out.1) | copy-start | bytes 1572868

commit v4 on v3

--- a/solution.py
+++ b/solution.py
@@ -37,7 +37,7 @@
     feat, wq_hbm, wk_hbm, wv_hbm, bits, slots, counts, ids,
     kb, vt, q_out, ints_out, dq_out, self_score, self_value,
     fbuf, wq, wk, wv, wqt, wkt, wvt, dq, ints, got,
-    ring_send, ring_recv, sib_send, sib_recv, z_send, z_recv, i_send, i_recv, in_sem,
+    ring_send, ring_recv, sib_send, sib_recv, z_send, z_recv, i_send, i_recv, x_send, x_recv, in_sem,
 ):
     x, y, c, z = place()
     me = dst_index(x, y, c)
@@ -66,7 +66,7 @@
         ints[b, 0:1, :] = bits[b : b + 1, :]
         ints[b, 1:2, 0:SLOTS] = slots[b]
         ints[b, 2:3, :] = ids[b % 2 : b % 2 + 1, :]
-        ints[b, 3:4, :] = jnp.broadcast_to(counts[b : b + 1, :], (1, BLK))
+        ints[b, 3:4, :] = jnp.broadcast_to(counts[0:1, b : b + 1], (1, BLK))
     loads[0].wait()
     pl.semaphore_wait(barrier, len(peers))
 
@@ -107,37 +107,37 @@
         arrive(row, 2)
         go(leg(row, 5, 1))
 
-    def share(*places):
-        for i, j in places:
-            b = blk(c, i, j)
-            go(remote(fbuf.at[b], fbuf.at[b], sib_send.at[i, j], sib_recv.at[i, j], (sibling, z)))
-
-    def shared(*places):
-        for i, j in places:
-            b = blk(1 - c, i, j)
-            remote(fbuf.at[b], fbuf.at[b], sib_send.at[i, j], sib_recv.at[i, j], (sibling, z)).wait_recv()
-
-    def project(b):
+    def handed(core, i, j):
+        b = blk(core, i, j)
+        return [
+            remote(r.at[b], r.at[b], sib_send.at[i, j, n], sib_recv.at[i, j, n], (sibling, z))
+            for n, r in enumerate((kb, vt))
+        ]
+
+    def project(i, j):
+        b = blk(c, i, j)
+        keys, values = handed(c, i, j)
         f = fbuf[b]
         kb[b] = jnp.dot(f, wk[...], preferred_element_type=F32).astype(BF)
+        keys.start()
         v = nt(wvt[...], f).astype(BF)
         vt[b, 0] = v[:, :BLK]
         vt[b, 1] = v[:, BLK:]
-
-    def project_many(core, *places):
+        values.start()
+
+    def project_many(*places):
         code = 0
         for i, j in reversed(places):
             code = code * 16 + 4 * i + j
 
         def body(e, code):
-            project(blk(core, code % 16 // 4, code % 4))
+            project(code % 16 // 4, code % 4)
             return code // 16
 
         lax.fori_loop(0, len(places), body, jnp.int32(code))
 
     spread(0)
     spread(1)
-    share((0, 0))
     for dy in range(4):
         for dc in range(2):
             s = (2 * y + dy) % 4
@@ -161,44 +161,35 @@
     arrive(0, 1, 3)
     spread(4)
     spread(2)
-    share((3, 0), (1, 0))
     arrive(0, 4, 5)
     spread(3)
-    share((2, 0))
     arrive(1, 1, 3)
-    share((0, 3), (0, 1))
     arrive(1, 4, 5)
-    share((0, 2))
-    shared((0, 0))
-    project(me)
-    project(sibling)
-    project_many(c, (1, 0), (3, 0), (0, 1))
-    shared((1, 0), (3, 0), (0, 1), (0, 3), (2, 0), (0, 2))
 
     yy = (z - y + 4) % 4
 
-    def plane_rows(cc):
-        return fbuf.at[dst_index(x, yy, cc), pl.ds(pl.multiple_of(flip(c, cc) * BLK, BLK), BLK)]
-
-    for first in range(2):
-        for up, to in ((0, zup), (1, zdown)):
-            cc = flip(first, up)
-            go(remote(plane_rows(cc), dq.at[z, cc], z_send.at[up, cc], z_recv.at[up, cc], (me, to)))
-    own_copies = [pltpu.make_async_copy(plane_rows(cc), dq.at[z, cc], z_recv.at[3, cc]) for cc in range(2)]
-    for copy in own_copies:
-        copy.start()
-
+    def plane_rows(half):
+        return fbuf.at[dst_index(x, yy, c), pl.ds(half * BLK, BLK)]
+
+    cross = remote(plane_rows(1), dq.at[z, c], x_send.at[0], x_recv.at[0], (sibling, z))
+    go(cross)
+    own_copy = pltpu.make_async_copy(plane_rows(0), dq.at[z, c], in_sem.at[4])
+    own_copy.start()
+    for up, to in ((0, zup), (1, zdown)):
+        go(remote(plane_rows(0), dq.at[z, c], z_send.at[up, c], z_recv.at[up, c], (me, to)))
+    project_many((0, 0), (1, 0))
+    remote(dq.at[z, 1 - c], dq.at[z, 1 - c], x_send.at[0], x_recv.at[0], (sibling, z)).wait_recv()
+    for up, to in ((0, zup), (1, zdown)):
+        go(remote(dq.at[z, 1 - c], dq.at[z, 1 - c], z_send.at[up, 1 - c], z_recv.at[up, 1 - c], (me, to)))
+    project_many((3, 0), (0, 1))
     forward(4)
     forward(2)
-    project_many(c, (0, 3), (2, 0), (0, 2))
     wqt[...] = wq[...].T
     wkt[...] = wk[...].T
+    project_many((0, 3), (2, 0), (0, 2))
+    forward(3)
     arrive(4, 1, 3)
-    share((3, 3), (3, 1))
     arrive(2, 1, 3)
-    share((1, 3), (1, 1))
-    project_many(1 - c, (1, 0), (3, 0))
-    forward(3)
 
     def z_leg(up, cc, frm):
         return remote(dq.at[frm, cc], dq.at[frm, cc], z_send.at[up, cc], z_recv.at[up, cc], (me, zup))
@@ -207,10 +198,8 @@
     go(remote(dq.at[zdown, 0], dq.at[zdown, 0], z_send.at[2, 0], z_recv.at[2, 0], (me, zup)))
     z_leg(1, 1, zup).wait_recv()
     go(remote(dq.at[zup, 1], dq.at[zup, 1], z_send.at[2, 1], z_recv.at[2, 1], (me, zdown)))
-    project_many(1 - c, (0, 1), (0, 3), (2, 0), (0, 2))
-    project_many(c, (1, 1), (1, 3), (3, 1), (3, 3))
-    for copy in own_copies:
-        copy.wait()
+    project_many((1, 1), (1, 3), (3, 1), (3, 3))
+    own_copy.wait()
 
     def query(s, cc):
         q = nt(wqt[...], dq[s, cc]).astype(BF)
@@ -222,12 +211,6 @@
 
     z_leg(0, 1, zdown).wait_recv()
     z_leg(1, 0, zup).wait_recv()
-    arrive(4, 4, 5)
-    share((3, 2))
-    arrive(2, 4, 5)
-    share((1, 2))
-    shared((1, 1), (1, 3), (3, 1), (3, 3))
-    project_many(1 - c, (1, 1), (1, 3), (3, 1), (3, 3))
     lax.fori_loop(0, 6, queries, 0)
     for cc in range(2):
         f = dq[z, cc]
@@ -248,22 +231,24 @@
                     got.at[slot], got.at[slot], i_send.at[dy, dc], i_recv.at[dy, dc], (sibling, z)
                 ).wait_recv()
     ints_out[...] = got[...]
-    project_many(c, (1, 2), (3, 2))
+    arrive(4, 4, 5)
+    arrive(2, 4, 5)
+    project_many((3, 2), (1, 2))
     arrive(3, 1, 3)
-    share((2, 3), (2, 1))
+    project_many((2, 1), (2, 3))
     far = (z + 2) % 4
     for cc in range(2):
         z_leg(2, cc, far).wait_recv()
     for cc in range(2):
         query(far, cc)
-    shared((1, 2), (3, 2))
-    project_many(1 - c, (1, 2), (3, 2))
-    project_many(c, (2, 1), (2, 3))
     arrive(3, 4, 5)
-    share((2, 2))
-    project_many(c, (2, 2))
-    shared((2, 1), (2, 3), (2, 2))
-    project_many(1 - c, (2, 1), (2, 3), (2, 2))
+    project(2, 2)
+    for i in range(4):
+        for j in range(4):
+            for copy in handed(1 - c, i, j):
+                copy.wait_recv()
+            for copy in handed(c, i, j):
+                copy.wait_send()
     for copy in sent:
         copy.wait_send()
 
@@ -278,7 +263,7 @@
             pltpu.VMEM((32, ROWS, WIDTH), BF),
             pltpu.VMEM((32, 2, WIDTH, BLK), BF),
             pltpu.VMEM((8, WIDTH, BLK), BF),
-            jax.ShapeDtypeStruct((8, 8, BLK), I32),
+            pltpu.VMEM((8, 8, BLK), I32),
             pltpu.VMEM((2, BLK, WIDTH), BF),
             pltpu.VMEM((2, HEADS, BLK), F32),
             pltpu.VMEM((2, WIDTH, BLK), BF),
@@ -291,8 +276,8 @@
             pltpu.VMEM((4, 2, BLK, WIDTH), BF),
             pltpu.VMEM((8, 8, BLK), I32),
             pltpu.VMEM((8, 8, BLK), I32),
-            dma((5, 6)), dma((5, 6)), dma((4, 4)), dma((4, 4)),
-            dma((3, 2)), dma((4, 2)), dma((4, 2)), dma((4, 2)), dma((4,)),
+            dma((5, 6)), dma((5, 6)), dma((4, 4, 2)), dma((4, 4, 2)),
+            dma((3, 2)), dma((3, 2)), dma((4, 2)), dma((4, 2)), dma((1,)), dma((1,)), dma((5,)),
         ],
         compiler_params=pltpu.CompilerParams(
             collective_id=0, has_side_effects=True, vmem_limit_bytes=44 << 20
@@ -302,11 +287,13 @@
 
 
 def attention_kernel(
-    lists, qt, bits, self_score, self_value, kb, vt,
+    qt, bits, self_score, self_value, kb, vt,
     acc_out, stat_out,
-    et, rhs, acc, m, l, sched, sx, sy, mx, my,
+    lists, list_sem, et, rhs, acc, m, l, sched, sx, sy, mx, my,
 ):
     x, y, c, z = place()
+    fetch = pltpu.make_async_copy(bits, lists, list_sem)
+    fetch.start()
     lane = lax.broadcasted_iota(I32, (BLK, BLK), 1)
     row = lax.broadcasted_iota(I32, (BLK, BLK), 0)
     for ph in range(15):
@@ -332,6 +319,7 @@
 
         return lax.fori_loop(0, (count + 1) // 2, inner, n)
 
+    fetch.wait()
     steps = lax.fori_loop(0, 8, build, 0)
     for extra in range(2):
         for f in range(5):
@@ -418,16 +406,17 @@
 
 def attention_call(ints, qt, self_score, self_value, kb, vt):
     vm = pl.BlockSpec(memory_space=pltpu.VMEM)
-    sm = pl.BlockSpec(memory_space=pltpu.SMEM)
     return pl.pallas_call(
         attention_kernel,
         out_shape=(
             pltpu.VMEM((8, WIDTH, BLK), BF),
             pltpu.VMEM((8, 16, BLK), F32),
         ),
-        in_specs=[sm, vm, vm, vm, vm, vm, vm],
+        in_specs=[vm] * 6,
         out_specs=(vm, vm),
         scratch_shapes=[
+            pltpu.SMEM((8, 8, BLK), I32),
+            pltpu.SemaphoreType.DMA,
             pltpu.VMEM((16, BLK, BLK), BF),
             pltpu.VMEM((8, 4, 256, 256), BF),
             pltpu.VMEM((8, WIDTH, BLK), F32),
@@ -441,7 +430,7 @@
         ],
         compiler_params=pltpu.CompilerParams(vmem_limit_bytes=24 << 20),
         name="block_attention",
-    )(ints, qt, ints, self_score, self_value, kb, vt)
+    )(qt, ints, self_score, self_value, kb, vt)
 
 
 def merge_kernel(
@@ -619,7 +608,7 @@
 def shards(features, w_query, w_key, w_value, w_out, node_bits, block_src, block_count, graph_ids):
     kb, vt, qt, got, dq, self_score, self_value = gather_call(
         features, w_query, w_key, w_value,
-        node_bits.reshape(8, BLK), block_src, block_count, graph_ids.reshape(2, BLK),
+        node_bits.reshape(8, BLK), block_src, block_count.reshape(1, 8), graph_ids.reshape(2, BLK),
     )
     acc, stat = attention_call(
         got, qt, self_score, self_value, kb.reshape(64, BLK, WIDTH), vt.reshape(64, WIDTH, BLK)

time: 109 us -> 95.5 us (0.88)
  Pallas kernels: 105 us -> 93.4 us
  local copies, waits for them, and re-layouts: 3.38 us -> 1.31 us
    pallas_call x1, Pallas kernels: 47.4 us -> 34.7 us  [merge_call(): pl.pallas_call(merge_kernel, out_shape=(jax.ShapeDtypeStruct((ROWS, WIDTH...]
    pallas_call x1, Pallas kernels: 13.5 us -> 19.8 us  [attention_call(): pl.pallas_call(attention_kernel, out_shape=(pltpu.VMEM((8, WIDTH, BLK), B...]
    pallas_call x1, Pallas kernels: 43.7 us -> 38.9 us  [gather_call(): pl.pallas_call(gather_kernel, out_shape=(pltpu.VMEM((32, ROWS, WIDTH), BF...]
    unnamed x7 -> x4, local copies, waits for them, and re-layouts: 3.38 us -> 1.31 us
where the time goes in v4:
time: 95.5 us; the launch traced here: 95.3 us
  Pallas kernels  93.4 us (98%)
  local copies, waits for them, and re-layouts  1.31 us (1%)
    pallas_call x1, Pallas kernels, gather_call(): pl.pallas_call(gather_kernel, out_shape=(pltpu.VMEM((32, ROWS, WIDTH), BF...  38.9 us
    pallas_call x1, Pallas kernels, merge_call(): pl.pallas_call(merge_kernel, out_shape=(jax.ShapeDtypeStruct((ROWS, WIDTH...  34.7 us
    pallas_call x1, Pallas kernels, attention_call(): pl.pallas_call(attention_kernel, out_shape=(pltpu.VMEM((8, WIDTH, BLK), B...  19.8 us

profile of v4, /device:TPU:1, one launch (start us, length us, event | category | flops | bytes accessed | tf_op | source)
XLA Modules:
  0.0 95.3 jit_solution(12558918377867567928)
XLA Ops:
  0.6 38.9 %gather_project.1 = (bf16[32,256,512]{2,1,0:T(8,128)(2,1)S(1)}, bf16[32,2,512,128]{3,2,1,0:T(8,128)(2,1)S(1)}, bf16[8,512,128]{2,1,0:T(8,128)(2,1)S(1)}, s32[8,8...) custom-call(bf16[256,512]{1,0:T(8,128)(2,1)} %feat.1, ...), custom_call_target="tpu_custom_call" | custom-call | tf_op jit(solution)/shard_map/gather_project/pallas_call | solution.py:260
  39.6 0.0 copy-start
  39.6 19.8 %block_attention.1 = (bf16[8,512,128]{2,1,0:T(8,128)(2,1)S(1)}, f32[8,16,128]{2,1,0:T(8,128)S(1)}) custom-call(bf16[8,512,128]{2,1,0:T(8,128)(2,1)S(1)} %get-tuple-element.11.qt, s32[8,8,128]{2,1,0:T(8,128)S(1)} %get-tuple-element.12.bits.ids, f32[2,8,128]{2,1,0:T(8,128)S(1)} %get-tuple-element.13.self_score, ...), custom_call_target="tpu_custom_call" | custom-call | tf_op jit(solution)/shard_map/block_attention/pallas_call | solution.py:409
  59.4 0.0 copy-done
  59.4 34.7 %merge_project_pool.1 = (bf16[256,512]{1,0:T(8,128)(2,1)S(1)}, f32[4,512]{1,0:T(4,128)S(1)}) custom-call(bf16[8,512,128]{2,1,0:T(8,128)(2,1)S(1)} %get-tuple-element.17.acc, f32[8,16,128]{2,1,0:T(8,128)S(1)} %get-tuple-element.18.stat, bf16[2,128,512]{2,1,0:T(8,128)(2,1)S(1)} %get-tuple-element.19.dq, s32[8,8,128]{2,1,0:T(8,128)S(1)} %get-tuple-element.12.bits.ids, ...), custom_call_target="tpu_custom_call" | custom-call | tf_op jit(solution)/shard_map/merge_project_pool/pallas_call | solution.py:579
  94.0 0.7 copy.13
  94.7 0.6 copy.14
Async XLA Ops:
  39.6 19.8 %copy-start = (bf16[512,512]{1,0:T(8,128)(2,1)S(1)}, bf16[512,512]{1,0:T(8,128)(2,1)}, u32[]{:S(2)}) copy-start(bf16[512,512]{1,0:T(8,128)(2,1)} %w_out.1) | copy-start | bytes 1572868

commit v5 on v4

--- a/solution.py
+++ b/solution.py
@@ -35,7 +35,7 @@
 
 def gather_kernel(
     feat, wq_hbm, wk_hbm, wv_hbm, bits, slots, counts, ids,
-    kb, vt, q_out, ints_out, dq_out, self_score, self_value,
+    kb, vt, q_out, ints_out, dq_out, self_score, self_value, et,
     fbuf, wq, wk, wv, wqt, wkt, wvt, dq, ints, got,
     ring_send, ring_recv, sib_send, sib_recv, z_send, z_recv, i_send, i_recv, x_send, x_recv, in_sem,
 ):
@@ -153,6 +153,11 @@
                         (dst_index(x, y + dy, flip(c, dc)), z),
                     )
                 )
+    lane = lax.broadcasted_iota(I32, (BLK, BLK), 1)
+    row = lax.broadcasted_iota(I32, (BLK, BLK), 0)
+    for ph in range(15):
+        et[ph] = jnp.where((row + 2 * ph) % 30 == lane, 1.0, 0.0).astype(BF)
+    et[15] = jnp.where(lane == 31, 1.0, 0.0).astype(BF)
     forward(0)
     forward(1)
     for copy in loads[1:]:
@@ -267,9 +272,10 @@
             pltpu.VMEM((2, BLK, WIDTH), BF),
             pltpu.VMEM((2, HEADS, BLK), F32),
             pltpu.VMEM((2, WIDTH, BLK), BF),
+            pltpu.VMEM((16, BLK, BLK), BF),
         ),
         in_specs=[hbm] * 4 + [vm] * 4,
-        out_specs=(vm,) * 7,
+        out_specs=(vm,) * 8,
         scratch_shapes=[
             pltpu.VMEM((32, ROWS, WIDTH), BF),
             *[pltpu.VMEM((WIDTH, WIDTH), BF)] * 6,
@@ -287,18 +293,13 @@
 
 
 def attention_kernel(
-    qt, bits, self_score, self_value, kb, vt,
+    qt, bits, self_score, self_value, kb, vt, et,
     acc_out, stat_out,
-    lists, list_sem, et, rhs, acc, m, l, sched, sx, sy, mx, my,
+    lists, list_sem, rhs, acc, m, l, sched, sx, sy, mx, my,
 ):
     x, y, c, z = place()
     fetch = pltpu.make_async_copy(bits, lists, list_sem)
     fetch.start()
-    lane = lax.broadcasted_iota(I32, (BLK, BLK), 1)
-    row = lax.broadcasted_iota(I32, (BLK, BLK), 0)
-    for ph in range(15):
-        et[ph] = jnp.where((row + 2 * ph) % 30 == lane, 1.0, 0.0).astype(BF)
-    et[15] = jnp.where(lane == 31, 1.0, 0.0).astype(BF)
 
     def phase(g):
         return (4 * ((g // 2) * 8 + 2 * z + g % 2)) % 15
@@ -370,7 +371,7 @@
         tops[2 * p] = top[:, :128]
         tops[2 * p + 1] = top[:, 128:]
 
-    def head(i, cur, tops, h):
+    def soften(i, cur, tops, h):
         b = sched[0, i]
         p, side = h // 2, h % 2
         old = m[b, h : h + 1, :]
@@ -379,16 +380,23 @@
         w = jnp.exp(cur[p, :, 128 * side : 128 * side + 128] - top)
         m[b, h : h + 1, :] = top
         l[b, h : h + 1, :] = l[b, h : h + 1, :] * factor + jnp.sum(w, axis=0, keepdims=True)
-        rows = slice(64 * h, 64 * h + 64)
+        return w.astype(BF), factor
+
+    def pair(i, cur, tops, p):
+        b = sched[0, i]
+        made = [soften(i, cur, tops, 2 * p + side) for side in range(2)]
+        rows = slice(128 * p, 128 * p + 128)
         v = jnp.concatenate([vt[sched[1, i], rows, :], vt[sched[2, i], rows, :]], 1)
-        o = jnp.dot(v, w.astype(BF), preferred_element_type=F32)
-        acc[b, rows, :] = acc[b, rows, :] * factor + o
+        o = jnp.dot(v, jnp.concatenate([w for w, _ in made], 1), preferred_element_type=F32)
+        for side in range(2):
+            rows = slice(128 * p + 64 * side, 128 * p + 64 * side + 64)
+            block = o[64 * side : 64 * side + 64, 128 * side : 128 * side + 128]
+            acc[b, rows, :] = acc[b, rows, :] * made[side][1] + block
 
     def step(i, cur, tops, nxt, next_tops):
         for p in range(4):
             scores(i + 1, nxt, next_tops, p)
-            head(i, cur, tops, 2 * p)
-            head(i, cur, tops, 2 * p + 1)
+            pair(i, cur, tops, p)
 
     for p in range(4):
         scores(0, sx, mx, p)
@@ -404,7 +412,7 @@
     stat_out[:, 8:16, :] = l[...]
 
 
-def attention_call(ints, qt, self_score, self_value, kb, vt):
+def attention_call(ints, qt, self_score, self_value, kb, vt, et):
     vm = pl.BlockSpec(memory_space=pltpu.VMEM)
     return pl.pallas_call(
         attention_kernel,
@@ -412,12 +420,11 @@
             pltpu.VMEM((8, WIDTH, BLK), BF),
             pltpu.VMEM((8, 16, BLK), F32),
         ),
-        in_specs=[vm] * 6,
+        in_specs=[vm] * 7,
         out_specs=(vm, vm),
         scratch_shapes=[
             pltpu.SMEM((8, 8, BLK), I32),
             pltpu.SemaphoreType.DMA,
-            pltpu.VMEM((16, BLK, BLK), BF),
             pltpu.VMEM((8, 4, 256, 256), BF),
             pltpu.VMEM((8, WIDTH, BLK), F32),
             pltpu.VMEM((8, HEADS, BLK), F32),
@@ -430,7 +437,7 @@
         ],
         compiler_params=pltpu.CompilerParams(vmem_limit_bytes=24 << 20),
         name="block_attention",
-    )(qt, ints, self_score, self_value, kb, vt)
+    )(qt, ints, self_score, self_value, kb, vt, et)
 
 
 def merge_kernel(
@@ -520,7 +527,7 @@
             for n, k in enumerate(slots):
                 o = o + acc_got[k, rows, :].astype(F32) * factors[n + 1][h : h + 1, :]
             pieces.append(o)
-        att = jnp.concatenate(pieces, 0).T.astype(BF)
+        att = jnp.concatenate(pieces, 0).astype(BF).T
         mixed = jnp.dot(att, w_out[...], preferred_element_type=F32)
         new = (dq[cc].astype(F32) + mixed).astype(BF)
         made[cc] = new
@@ -606,12 +613,12 @@
 
 
 def shards(features, w_query, w_key, w_value, w_out, node_bits, block_src, block_count, graph_ids):
-    kb, vt, qt, got, dq, self_score, self_value = gather_call(
+    kb, vt, qt, got, dq, self_score, self_value, et = gather_call(
         features, w_query, w_key, w_value,
         node_bits.reshape(8, BLK), block_src, block_count.reshape(1, 8), graph_ids.reshape(2, BLK),
     )
     acc, stat = attention_call(
-        got, qt, self_score, self_value, kb.reshape(64, BLK, WIDTH), vt.reshape(64, WIDTH, BLK)
+        got, qt, self_score, self_value, kb.reshape(64, BLK, WIDTH), vt.reshape(64, WIDTH, BLK), et
     )
     return merge_call(acc, stat, dq, got, w_out)
 

time: 95.5 us -> 92.5 us (0.969); the launches traced: 95.3 us -> 91.1 us
  Pallas kernels: 93.4 us -> 89.1 us
    pallas_call x1, Pallas kernels: 34.7 us -> 29.1 us  [merge_call(): pl.pallas_call(merge_kernel, out_shape=(jax.ShapeDtypeStruct((ROWS, WIDTH...]
    pallas_call x1, Pallas kernels: 19.8 us -> 21.1 us  [attention_call(): pl.pallas_call(attention_kernel, out_shape=(pltpu.VMEM((8, WIDTH, BLK), B...]
where the time goes in v5:
time: 92.5 us; the launch traced here: 91.1 us
  Pallas kernels  89.1 us (96%)
  local copies, waits for them, and re-layouts  1.31 us (1%)
    pallas_call x1, Pallas kernels, gather_call(): pl.pallas_call(gather_kernel, out_shape=(pltpu.VMEM((32, ROWS, WIDTH), BF...  38.9 us
    pallas_call x1, Pallas kernels, merge_call(): pl.pallas_call(merge_kernel, out_shape=(jax.ShapeDtypeStruct((ROWS, WIDTH...  29.1 us
    pallas_call x1, Pallas kernels, attention_call(): pl.pallas_call(attention_kernel, out_shape=(pltpu.VMEM((8, WIDTH, BLK), B...  21.1 us

profile of v5, /device:TPU:1, one launch (start us, length us, event | category | flops | bytes accessed | tf_op | source)
XLA Modules:
  0.0 91.1 jit_solution(7666765811652370402)
XLA Ops:
  0.6 38.9 %gather_project.1 = (bf16[32,256,512]{2,1,0:T(8,128)(2,1)S(1)}, bf16[32,2,512,128]{3,2,1,0:T(8,128)(2,1)S(1)}, bf16[8,512,128]{2,1,0:T(8,128)(2,1)S(1)}, s32[8,8...) custom-call(bf16[256,512]{1,0:T(8,128)(2,1)} %feat.1, ...), custom_call_target="tpu_custom_call" | custom-call | tf_op jit(solution)/shard_map/gather_project/pallas_call | solution.py:265
  39.6 0.0 copy-start
  39.6 21.1 %block_attention.1 = (bf16[8,512,128]{2,1,0:T(8,128)(2,1)S(1)}, f32[8,16,128]{2,1,0:T(8,128)S(1)}) custom-call(bf16[8,512,128]{2,1,0:T(8,128)(2,1)S(1)} %get-tuple-element.12.qt, s32[8,8,128]{2,1,0:T(8,128)S(1)} %get-tuple-element.13.bits.ids, f32[2,8,128]{2,1,0:T(8,128)S(1)} %get-tuple-element.14.self_score, ...), custom_call_target="tpu_custom_call" | custom-call | tf_op jit(solution)/shard_map/block_attention/pallas_call | solution.py:417
  60.7 0.0 copy-done
  60.7 29.1 %merge_project_pool.1 = (bf16[256,512]{1,0:T(8,128)(2,1)S(1)}, f32[4,512]{1,0:T(4,128)S(1)}) custom-call(bf16[8,512,128]{2,1,0:T(8,128)(2,1)S(1)} %get-tuple-element.19.acc, f32[8,16,128]{2,1,0:T(8,128)S(1)} %get-tuple-element.20.stat, bf16[2,128,512]{2,1,0:T(8,128)(2,1)S(1)} %get-tuple-element.21.dq, s32[8,8,128]{2,1,0:T(8,128)S(1)} %get-tuple-element.13.bits.ids, ...), custom_call_target="tpu_custom_call" | custom-call | tf_op jit(solution)/shard_map/merge_project_pool/pallas_call | solution.py:586
  89.8 0.7 copy.13
  90.5 0.6 copy.14
Async XLA Ops:
  39.6 21.1 %copy-start = (bf16[512,512]{1,0:T(8,128)(2,1)S(1)}, bf16[512,512]{1,0:T(8,128)(2,1)}, u32[]{:S(2)}) copy-start(bf16[512,512]{1,0:T(8,128)(2,1)} %w_out.1) | copy-start | bytes 1572868
